TPU v7x, 128 devices: a whole 4x4x4 slice. The times are simulated.
128 devices in a mesh: gx: 8 (over y_lo, z), gy: 16 (over x, y_hi, core).
Axes of the slice: x: 4, y: 4 (y_hi: 2, y_lo: 2; y = y_hi * 2 + y_lo), z: 4, core: 2. Of those that a mesh axis runs over, the one named last changes fastest.
Arguments:
- adjoint: bfloat16 [600, 512, 1024], P(None, 'gy', 'gx'), may hold values from -48 to 48
- seafloor_depth: float32 [512, 1024], P('gy', 'gx'), may hold values from 0.5 to 2
- sensor_row: int32 [600], replicated, may hold values from 0 to 1023
- sensor_column: int32 [600], replicated, may hold values from 0 to 511
- noise_sigma: float32 [600], replicated, may hold values from 0.15 to 0.6
Outputs:
- gain_field: bfloat16 [600, 512, 1024], P(None, 'gy', 'gx')
All inputs are finite; a program needn't handle non-finite values. Where the computation divides by a largest or mean magnitude, that divisor is 1e-20 or more.
Results may differ from a plain program's by a relative error of at most 0.0052.
The roundings to bfloat16 on the way count: a program that leaves them out, or rounds other values in their place, can miss the bound.
Values may be sent and summed in bfloat16 or wider, within the bound.
A program may use at most 128 MiB of HBM per device.

v0:
```python
import jax
import jax.numpy as jnp
from jax import lax
from jax.sharding import PartitionSpec as P

SWEEPS = 4
ITERS = 4


diffusion_step = 0.06


def over_pieces(shard, axis):
    pieces = lax.all_gather(shard, axis)
    return pieces.sum(axis=0)


def extended(block, sides, width):
    for axis, dim in sides:
        count = lax.axis_size(axis)
        forward = [(i, i + 1) for i in range(count - 1)]
        backward = [(target, source) for source, target in forward]
        low = lax.ppermute(
            lax.slice_in_dim(block, block.shape[dim] - width, None, axis=dim), axis, forward
        )
        high = lax.ppermute(lax.slice_in_dim(block, 0, width, axis=dim), axis, backward)
        block = jnp.concatenate([low, block, high], axis=dim)
    return block


def diffuse(padded, depth_padded):
    centre = depth_padded[1:-1, 1:-1]
    north_face = 0.5 * (centre + depth_padded[1:-1, 2:])
    south_face = 0.5 * (centre + depth_padded[1:-1, :-2])
    east_face = 0.5 * (centre + depth_padded[2:, 1:-1])
    west_face = 0.5 * (centre + depth_padded[:-2, 1:-1])
    middle = padded[:, 1:-1, 1:-1]
    face_flux = north_face * (padded[:, 1:-1, 2:] - middle)
    face_flux = face_flux + south_face * (padded[:, 1:-1, :-2] - middle)
    face_flux = face_flux + east_face * (padded[:, 2:, 1:-1] - middle)
    face_flux = face_flux + west_face * (padded[:, :-2, 1:-1] - middle)
    return middle + diffusion_step * face_flux


def matmul_highest(left, right):
    return jnp.dot(left, right, precision=lax.Precision.HIGHEST, preferred_element_type=jnp.float32)


def local(adjoint, seafloor_depth, sensor_row, sensor_column, noise_sigma):
    sensors, tile_columns, tile_rows = adjoint.shape
    column_offset = lax.axis_index("gy") * tile_columns
    row_offset = lax.axis_index("gx") * tile_rows
    pick_column = (
        sensor_column[:, None] - column_offset == jnp.arange(tile_columns)[None, :]
    ).astype(jnp.float32)
    pick_row = (sensor_row[:, None] - row_offset == jnp.arange(tile_rows)[None, :]).astype(
        jnp.float32
    )
    picked = jnp.sum(matmul_highest(pick_column, seafloor_depth) * pick_row, axis=1)
    under_sensor = over_pieces(picked, ("gx", "gy"))
    variance = noise_sigma * noise_sigma * under_sensor
    depth_padded = extended(seafloor_depth, (("gx", 1), ("gy", 0)), SWEEPS)
    inside = (depth_padded > 0.0).astype(jnp.float32)
    padded = extended(adjoint, (("gx", 2), ("gy", 1)), SWEEPS).astype(jnp.float32)
    padded_columns, padded_rows = depth_padded.shape
    for sweep_index in range(SWEEPS):
        depth_view = depth_padded[
            sweep_index : padded_columns - sweep_index, sweep_index : padded_rows - sweep_index
        ]
        mask_view = inside[
            sweep_index + 1 : padded_columns - sweep_index - 1,
            sweep_index + 1 : padded_rows - sweep_index - 1,
        ]
        padded = diffuse(padded, depth_view) * mask_view
    smoothed = padded.astype(jnp.bfloat16).reshape(sensors, tile_columns * tile_rows)
    inverse_cells = 1.0 / (tile_columns * tile_rows * lax.axis_size("gx") * lax.axis_size("gy"))
    partial_value = lax.dot_general(
        smoothed, smoothed, (((1,), (1,)), ((), ())), preferred_element_type=jnp.float32
    )
    gram = lax.psum(partial_value, ("gx", "gy"))
    operator = gram * inverse_cells + jnp.diag(variance)
    spectral_bound = jnp.max(jnp.sum(jnp.abs(operator), axis=1))
    inverse = jnp.eye(sensors, dtype=jnp.float32) / spectral_bound
    for _ in range(ITERS):
        inverse = 2.0 * inverse - matmul_highest(matmul_highest(inverse, operator), inverse)
    gain_field = jnp.dot(inverse.astype(jnp.bfloat16), smoothed, preferred_element_type=jnp.float32)
    return gain_field.astype(jnp.bfloat16).reshape(sensors, tile_columns, tile_rows)


def solution(mesh):
    in_specs = (P(None, "gy", "gx"), P("gy", "gx"), P(), P(), P())
    out_specs = P(None, "gy", "gx")
    return jax.shard_map(local, mesh=mesh, in_specs=in_specs, out_specs=out_specs, check_vma=False)
```

profile of v0, /device:TPU:1, one launch (start us, length us, event | category | flops | bytes accessed | tf_op | source)
XLA Modules:
  0.0 375.9 jit_solution(1823887705005888173)
XLA Ops:
  6.5 0.0 all-reduce.4.cloned.1.call-start
  6.5 0.9 fusion.79
  7.4 4.3 %collective-permute-start.4 = (f32[32,4]{1,0:T(8,128)S(1)}, f32[32,4]{1,0:T(8,128)S(1)}, u32[]{:S(2)}, u32[]{:S(2)}) collective-permute-start(f32[32,4]{1,0:T(8,128)S(1)} %get-tuple-element.33), channel_id=1, source_target_pairs={{0,16},{16,32},{32,48},{48,64},{64,80},{80,96},{96,112},{1,17},{17... | collective-permute-start | bytes 1544 | tf_op jit(solution)/shard_map/ppermute | solution.py:23
  11.8 1.3 collective-permute-start.5
  13.1 9.8 %fusion.78 = (bf16[600,32,4]{2,1,0:T(8,128)(2,1)}, bf16[600,32,4]{2,1,0:T(8,128)(2,1)}) fusion(bf16[600,32,128]{2,1,0:T(8,128)(2,1)} %param.5), kind=kLoop, calls=%fused_computation.134 | loop fusion | bytes 614400 | tf_op jit(solution)/shard_map/slice | solution.py:24
  22.9 5.5 %copy.19 = bf16[600,32,4]{0,1,2:T(8,128)(2,1)S(1)} copy(bf16[600,32,4]{2,1,0:T(8,128)(2,1)} %get-tuple-element.11) | data formatting | bytes 307200
  28.4 4.2 %collective-permute-start = (bf16[600,32,4]{0,1,2:T(8,128)(2,1)S(1)}, bf16[600,32,4]{0,1,2:T(8,128)(2,1)S(1)}, u32[]{:S(2)}, u32[]{:S(2)}) collective-permute-start(bf16[600,32,4]{0,1,2:T(8,128)(2,1)S(1)} %copy.19), channel_id=1, source_target_pairs={{0,16},{16,32},{32,48},{48,64},{64,80},{80,96},{96,112},{1,17},{17... | collective-permute-start | bytes 460808 | tf_op jit(solution)/shard_map/ppermute | solution.py:23
  32.6 5.5 %copy.20 = bf16[600,32,4]{0,1,2:T(8,128)(2,1)S(1)} copy(bf16[600,32,4]{2,1,0:T(8,128)(2,1)} %get-tuple-element.12) | data formatting | bytes 307200
  38.1 1.3 collective-permute-start.1
  39.4 0.0 collective-permute-done.4
  39.4 0.0 collective-permute-done.5
  39.5 0.1 pad_maximum_fusion.9
  39.5 6.0 %collective-permute-start.6 = (f32[4,136]{1,0:T(4,128)S(1)}, f32[4,136]{1,0:T(4,128)S(1)}, u32[]{:S(2)}, u32[]{:S(2)}) collective-permute-start(f32[4,136]{1,0:T(4,128)S(1)} %get-tuple-element.17), channel_id=1, source_target_pairs={{0,1},{1,2},{2,3},{3,4},{4,5},{5,6},{6,7},{7,8},{8,9},{9,10},{10,1... | collective-permute-start | bytes 6536 | tf_op jit(solution)/shard_map/ppermute | solution.py:23
  45.6 1.9 collective-permute-start.7
  47.5 0.5 fusion.49
  48.1 8.9 %copy.13 = bf16[600,32,128]{0,2,1:T(8,128)(2,1)} copy(bf16[600,32,128]{2,1,0:T(8,128)(2,1)} %param.5) | data formatting | bytes 9830400 | tf_op args[0]
  57.0 0.3 dynamic-update-slice
  57.3 0.0 collective-permute-done.6
  57.3 0.0 collective-permute-done.7
  57.3 0.1 compare_convert_fusion
  57.4 0.1 fusion.66
  57.5 0.1 slice.242
  57.6 0.1 slice.253
  57.6 0.1 slice.264
  57.7 0.1 slice.270
  57.8 0.1 pad_maximum_fusion.4
  57.9 0.0 collective-permute-done
  57.9 0.1 copy.12
  58.0 0.0 collective-permute-done.1
  58.0 0.1 copy.14
  58.1 0.0 slice-start.1
  58.1 1.8 pad_maximum_fusion.2
  60.0 5.1 %collective-permute-start.2 = (bf16[600,4,136]{0,2,1:T(8,128)(2,1)S(1)}, bf16[600,4,136]{0,2,1:T(8,128)(2,1)S(1)}, u32[]{:S(2)}, u32[]{:S(2)}) collective-permute-start(bf16[600,4,136]{0,2,1:T(8,128)(2,1)S(1)} %get-tuple-element.9), channel_id=1, source_target_pairs={{0,1},{1,2},{2,3},{3,4},{4,5},{5,6},{6,7},{7,8},{8,9},{9,10},{10,1... | collective-permute-start | bytes 1958408 | tf_op jit(solution)/shard_map/ppermute | solution.py:23
  65.1 2.1 collective-permute-start.3
  67.3 0.1 fusion.68
  67.4 0.1 fusion.62
  67.5 0.1 fusion.58
  67.6 12.9 %collective-permute-done.2 = bf16[600,4,136]{0,2,1:T(8,128)(2,1)S(1)} collective-permute-done((bf16[600,4,136]{0,2,1:T(8,128)(2,1)S(1)}, bf16[600,4,136]{0,2,1:T(8,128)(2,1)S(1)}, u32[]{:S(2)}, u32[]{:S(2)}) %collective-permute-start.2) | collective-permute-done | bytes 652832 | tf_op jit(solution)/shard_map/ppermute | solution.py:23
  80.5 0.0 collective-permute-done.3
  80.5 2.3 maximum_convert_fusion
  82.8 12.2 %fusion.4 = f32[600,38,134]{0,2,1:T(8,128)} fusion(f32[600,40,136]{0,2,1:T(8,128)S(1)} %maximum_convert_fusion, f32[38,134]{1,0:T(8,128)S(1)} %slice.242, f32[38,134]{1,0:T(8,128)S(1)} %get-tuple-element.28, f32[38,134]{1,0:T(8,128)S(1)} %get-tuple-element.29, f32[38,134]{1,0:T(8,128)S(1)} %get-tuple-element.30, f32[38,134]{1,0:T(8,128)S(1)} %get-tuple-element.27), kind=kLoop, calls=%fused_computation.5 | loop fusion | flops 42772800 | bytes 73426640 | tf_op jit(solution)/shard_map/mul | solution.py:74
  95.0 25.7 %fusion.14 = f32[600,36,132]{0,2,1:T(8,128)S(1)} fusion(f32[600,38,134]{0,2,1:T(8,128)} %fusion.4, f32[36,132]{1,0:T(8,128)S(1)} %slice.253, f32[36,132]{1,0:T(8,128)S(1)} %get-tuple-element.24, f32[36,132]{1,0:T(8,128)S(1)} %get-tuple-element.25, f32[36,132]{1,0:T(8,128)S(1)} %get-tuple-element.26, f32[36,132]{1,0:T(8,128)S(1)} %get-tuple-element.23), kind=kLoop, calls=%fused_computation.19 | loop fusion | flops 39916800 | bytes 68523840 | tf_op jit(solution)/shard_map/mul | solution.py:74
  120.7 10.8 %fusion.24 = f32[600,34,130]{0,2,1:T(8,128)} fusion(f32[600,36,132]{0,2,1:T(8,128)S(1)} %fusion.14, f32[34,130]{1,0:T(8,128)S(1)} %slice.264, f32[34,130]{1,0:T(8,128)S(1)} %get-tuple-element.21, f32[34,130]{1,0:T(8,128)S(1)} %get-tuple-element.20, f32[34,130]{1,0:T(8,128)S(1)} %get-tuple-element.22, f32[34,130]{1,0:T(8,128)S(1)} %get-tuple-element.19), kind=kLoop, calls=%fused_computation.33 | loop fusion | flops 37128000 | bytes 63736400 | tf_op jit(solution)/shard_map/mul | solution.py:74
  131.5 21.5 %fusion.35 = bf16[600,32,128]{0,2,1:T(8,128)(2,1)S(1)} fusion(f32[600,34,130]{0,2,1:T(8,128)} %fusion.24, f32[32,128]{1,0:T(8,128)S(1)} %slice.270, f32[32,128]{1,0:T(8,128)S(1)} %get-tuple-element.14, f32[32,128]{1,0:T(8,128)S(1)} %get-tuple-element.13, f32[32,128]{1,0:T(8,128)S(1)} %get-tuple-element.32, f32[32,128]{1,0:T(8,128)S(1)} %get-tuple-element.31), kind=kLoop, calls=%fused_computation.48 | loop fusion | flops 36864000 | bytes 54149120 | tf_op jit(solution)/shard_map/convert_element_type | solution.py:75
  153.0 2.3 copy-done.1
  155.3 5.2 %convolution_bitcast_fusion = f32[600,600]{1,0:T(8,128)} fusion(bf16[600,32,128]{0,2,1:T(8,128)(2,1)S(1)} %fusion.35), kind=kOutput, calls=%fused_computation.72 | convolution fusion | flops 2949120000 | bytes 6355200 | tf_op jit(solution)/shard_map/dot_general | solution.py:77
  160.5 0.0 all-reduce.4.cloned.1.call-update
  160.5 155.4 %all-reduce.4.cloned.1.call-done = (f32[76800]{0:T(1024)}, f32[600,600]{1,0:T(8,128)}) async-done(((f32[76800]{0:T(1024)}, f32[600,600]{1,0:T(8,128)}), (f32[76800]{0:T(1024)}, f32[600,600]{1,0:T(8,128)})) %all-reduce.4.cloned.1.call-update) | async-done | bytes 1747216
  315.9 1.3 reshape.33
  317.2 0.0 copy-done.6
  317.3 1.8 abs_reduce_fusion
  319.1 0.6 reduce_max.9
  320.4 5.9 %fusion.43 = f32[600,600]{1,0:T(8,128)S(1)} fusion(f32[]{:T(128)S(6)} %divide.3, f32[600,600]{1,0:T(8,128)} %get-tuple-element.6, f32[600]{0:T(1024)S(1)} %multiply_multiply_fusion), kind=kOutput, calls=%fused_computation.61 | convolution fusion | flops 2594160128 | bytes 2882404 | tf_op jit(solution)/shard_map/dot_general | solution.py:46
  326.3 5.0 %fusion.46 = f32[600,600]{1,0:T(8,128)S(1)} fusion(f32[600,600]{1,0:T(8,128)S(1)} %fusion.43, f32[]{:T(128)S(6)} %divide.3), kind=kOutput, calls=%fused_computation.65 | convolution fusion | flops 2594160128 | bytes 2880004 | tf_op jit(solution)/shard_map/dot_general | solution.py:46
  331.4 4.8 %fusion.77 = f32[600,600]{1,0:T(8,128)S(1)} fusion(f32[600,600]{1,0:T(8,128)S(1)} %fusion.46, f32[600,600]{1,0:T(8,128)S(1)} %copy-done, f32[600]{0:T(1024)S(1)} %multiply_multiply_fusion), kind=kOutput, calls=%fused_computation.133 | convolution fusion | flops 2593440000 | bytes 4322400 | tf_op jit(solution)/shard_map/dot_general | solution.py:46
  336.2 4.8 %multiply_subtract_fusion.1 = f32[600,600]{1,0:T(8,128)S(1)} fusion(f32[600,600]{1,0:T(8,128)S(1)} %fusion.46, f32[600,600]{1,0:T(8,128)S(1)} %fusion.77), kind=kOutput, calls=%fused_computation.68 | convolution fusion | flops 2592719872 | bytes 4320000 | tf_op jit(solution)/shard_map/dot_general | solution.py:46
  341.0 5.0 %fusion.76 = f32[600,600]{1,0:T(8,128)S(1)} fusion(f32[600,600]{1,0:T(8,128)S(1)} %multiply_subtract_fusion.1, f32[600,600]{1,0:T(8,128)S(1)} %copy-done, f32[600]{0:T(1024)S(1)} %multiply_multiply_fusion), kind=kOutput, calls=%fused_computation.132 | convolution fusion | flops 2593440000 | bytes 4322400 | tf_op jit(solution)/shard_map/dot_general | solution.py:46
  346.0 0.0 slice-start.2
  346.0 4.8 %multiply_subtract_fusion = f32[600,600]{1,0:T(8,128)S(1)} fusion(f32[600,600]{1,0:T(8,128)S(1)} %multiply_subtract_fusion.1, f32[600,600]{1,0:T(8,128)S(1)} %fusion.76), kind=kOutput, calls=%fused_computation.67 | convolution fusion | flops 2592719872 | bytes 4320000 | tf_op jit(solution)/shard_map/dot_general | solution.py:46
  350.8 0.0 slice-start.3
  350.8 5.0 %fusion.75 = f32[600,600]{1,0:T(8,128)S(1)} fusion(f32[600,600]{1,0:T(8,128)S(1)} %multiply_subtract_fusion, f32[600,600]{1,0:T(8,128)S(1)} %copy-done, f32[600]{0:T(1024)S(1)} %multiply_multiply_fusion), kind=kOutput, calls=%fused_computation.131 | convolution fusion | flops 2593440000 | bytes 4322400 | tf_op jit(solution)/shard_map/dot_general | solution.py:46
  355.8 4.7 %subtract_convert_fusion = bf16[600,600]{1,0:T(8,128)(2,1)S(1)} fusion(f32[600,600]{1,0:T(8,128)S(1)} %multiply_subtract_fusion, f32[600,600]{1,0:T(8,128)S(1)} %fusion.75), kind=kOutput, calls=%fused_computation.66 | convolution fusion | flops 2593080064 | bytes 3600000 | tf_op jit(solution)/shard_map/dot_general | solution.py:46
  360.6 4.3 %fusion.45 = bf16[75,8,32,128]{3,1,2,0:T(8,128)(2,1)S(1)} fusion(bf16[600,600]{1,0:T(8,128)(2,1)S(1)} %subtract_convert_fusion, bf16[600,4096]{0,1:T(8,128)(2,1)S(1)} %bitcast.25), kind=kOutput, calls=%fused_computation.64 | convolution fusion | flops 2951577600 | bytes 10550400 | tf_op jit(solution)/shard_map/dot_general | solution.py:86
  364.9 3.8 %copy.21 = bf16[75,8,32,128]{3,2,1,0:T(8,128)(2,1)} copy(bf16[75,8,32,128]{3,1,2,0:T(8,128)(2,1)S(1)} %fusion.45) | data formatting | bytes 9830400
  (23 shorter events, 0.1 us)
Async XLA Ops:
  6.5 309.4 %all-reduce.4.cloned.1.call-start = ((), (), s32[]{:S(2)}) async-start(), calls=%async_computation | async-start | bytes 3686400
  7.4 32.0 %collective-permute-start.4 = (f32[32,4]{1,0:T(8,128)S(1)}, f32[32,4]{1,0:T(8,128)S(1)}, u32[]{:S(2)}, u32[]{:S(2)}) collective-permute-start(f32[32,4]{1,0:T(8,128)S(1)} %get-tuple-element.33), channel_id=1, source_target_pairs={{0,16},{16,32},{32,48},{48,64},{64,80},{80,96},{96,112},{1,17},{17... | collective-permute-start | bytes 1544 | tf_op jit(solution)/shard_map/ppermute | solution.py:23
  11.8 27.7 %collective-permute-start.5 = (f32[32,4]{1,0:T(8,128)S(1)}, f32[32,4]{1,0:T(8,128)S(1)}, u32[]{:S(2)}, u32[]{:S(2)}) collective-permute-start(f32[32,4]{1,0:T(8,128)S(1)} %get-tuple-element.34), channel_id=1, source_target_pairs={{16,0},{32,16},{48,32},{64,48},{80,64},{96,80},{112,96},{17,1},{33... | collective-permute-start | bytes 1544 | tf_op jit(solution)/shard_map/ppermute | solution.py:26
  22.9 16.5 %copy-start.4 = (s32[600]{0:T(1024)S(1)}, s32[600]{0:T(1024)}, u32[]{:S(2)}) copy-start(s32[600]{0:T(1024)} %param.8) | copy-start | bytes 7204
  22.9 16.5 %copy-start.5 = (s32[600]{0:T(1024)S(1)}, s32[600]{0:T(1024)}, u32[]{:S(2)}) copy-start(s32[600]{0:T(1024)} %param.7) | copy-start | bytes 7204
  22.9 16.5 %copy-start.3 = (f32[32,128]{1,0:T(8,128)S(1)}, f32[32,128]{1,0:T(8,128)}, u32[]{:S(2)}) copy-start(f32[32,128]{1,0:T(8,128)} %param.6) | copy-start | bytes 49156
  28.4 29.5 %collective-permute-start = (bf16[600,32,4]{0,1,2:T(8,128)(2,1)S(1)}, bf16[600,32,4]{0,1,2:T(8,128)(2,1)S(1)}, u32[]{:S(2)}, u32[]{:S(2)}) collective-permute-start(bf16[600,32,4]{0,1,2:T(8,128)(2,1)S(1)} %copy.19), channel_id=1, source_target_pairs={{0,16},{16,32},{32,48},{48,64},{64,80},{80,96},{96,112},{1,17},{17... | collective-permute-start | bytes 460808 | tf_op jit(solution)/shard_map/ppermute | solution.py:23
  38.1 19.9 %collective-permute-start.1 = (bf16[600,32,4]{0,1,2:T(8,128)(2,1)S(1)}, bf16[600,32,4]{0,1,2:T(8,128)(2,1)S(1)}, u32[]{:S(2)}, u32[]{:S(2)}) collective-permute-start(bf16[600,32,4]{0,1,2:T(8,128)(2,1)S(1)} %copy.20), channel_id=1, source_target_pairs={{16,0},{32,16},{48,32},{64,48},{80,64},{96,80},{112,96},{17,1},{33... | collective-permute-start | bytes 460808 | tf_op jit(solution)/shard_map/ppermute | solution.py:26
  39.5 17.7 %collective-permute-start.6 = (f32[4,136]{1,0:T(4,128)S(1)}, f32[4,136]{1,0:T(4,128)S(1)}, u32[]{:S(2)}, u32[]{:S(2)}) collective-permute-start(f32[4,136]{1,0:T(4,128)S(1)} %get-tuple-element.17), channel_id=1, source_target_pairs={{0,1},{1,2},{2,3},{3,4},{4,5},{5,6},{6,7},{7,8},{8,9},{9,10},{10,1... | collective-permute-start | bytes 6536 | tf_op jit(solution)/shard_map/ppermute | solution.py:23
  45.6 11.7 %collective-permute-start.7 = (f32[4,136]{1,0:T(4,128)S(1)}, f32[4,136]{1,0:T(4,128)S(1)}, u32[]{:S(2)}, u32[]{:S(2)}) collective-permute-start(f32[4,136]{1,0:T(4,128)S(1)} %get-tuple-element.18), channel_id=1, source_target_pairs={{1,0},{2,1},{3,2},{4,3},{5,4},{6,5},{7,6},{8,7},{9,8},{10,9},{11,1... | collective-permute-start | bytes 6536 | tf_op jit(solution)/shard_map/ppermute | solution.py:26
  56.9 23.6 %slice-start = ((s8[5242880]{0:T(1024)(128)(4,1)}), s8[1048576]{0:T(1024)(128)(4,1)S(1)}, s32[]{:S(2)}) async-start(s8[5242880]{0:T(1024)(128)(4,1)} %bitcast.21), calls=%async_computation.1 | async-start | bytes 2097152
  57.3 25.6 %copy-start.2 = (f32[76800]{0:T(1024)}, f32[76800]{0:T(1024)S(1)}, u32[]{:S(2)}) copy-start(f32[76800]{0:T(1024)S(1)} %dynamic-update-slice) | copy-start | bytes 921604
  58.1 22.4 %slice-start.1 = ((s8[5242880]{0:T(1024)(128)(4,1)}), s8[4194304]{0:T(1024)(128)(4,1)S(1)}, s32[]{:S(2)}) async-start(s8[5242880]{0:T(1024)(128)(4,1)} %bitcast.21), calls=%async_computation.2 | async-start | bytes 8388608
  60.0 20.6 %collective-permute-start.2 = (bf16[600,4,136]{0,2,1:T(8,128)(2,1)S(1)}, bf16[600,4,136]{0,2,1:T(8,128)(2,1)S(1)}, u32[]{:S(2)}, u32[]{:S(2)}) collective-permute-start(bf16[600,4,136]{0,2,1:T(8,128)(2,1)S(1)} %get-tuple-element.9), channel_id=1, source_target_pairs={{0,1},{1,2},{2,3},{3,4},{4,5},{5,6},{6,7},{7,8},{8,9},{9,10},{10,1... | collective-permute-start | bytes 1958408 | tf_op jit(solution)/shard_map/ppermute | solution.py:23
  65.1 15.4 %collective-permute-start.3 = (bf16[600,4,136]{0,2,1:T(8,128)(2,1)S(1)}, bf16[600,4,136]{0,2,1:T(8,128)(2,1)S(1)}, u32[]{:S(2)}, u32[]{:S(2)}) collective-permute-start(bf16[600,4,136]{0,2,1:T(8,128)(2,1)S(1)} %get-tuple-element.10), channel_id=1, source_target_pairs={{1,0},{2,1},{3,2},{4,3},{5,4},{6,5},{7,6},{8,7},{9,8},{10,9},{11,1... | collective-permute-start | bytes 1958408 | tf_op jit(solution)/shard_map/ppermute | solution.py:26
  152.9 2.3 copy-start.1
  155.3 162.0 %copy-start.6 = (f32[600]{0:T(1024)S(1)}, f32[600]{0:T(1024)}, u32[]{:S(2)}) copy-start(f32[600]{0:T(1024)} %param.9) | copy-start | bytes 7204
  317.2 14.1 %copy-start = (f32[600,600]{1,0:T(8,128)S(1)}, f32[600,600]{1,0:T(8,128)}, u32[]{:S(2)}) copy-start(f32[600,600]{1,0:T(8,128)} %get-tuple-element.6) | copy-start | bytes 4320004
  346.0 14.6 %slice-start.2 = ((s8[5242880]{0:T(1024)(128)(4,1)}), s8[4194304]{0:T(1024)(128)(4,1)S(1)}, s32[]{:S(2)}) async-start(s8[5242880]{0:T(1024)(128)(4,1)} %bitcast.23), calls=%async_computation.3 | async-start | bytes 8388608
  350.8 9.8 %slice-start.3 = ((s8[5242880]{0:T(1024)(128)(4,1)}), s8[1048576]{0:T(1024)(128)(4,1)S(1)}, s32[]{:S(2)}) async-start(s8[5242880]{0:T(1024)(128)(4,1)} %bitcast.23), calls=%async_computation.4 | async-start | bytes 2097152
Sparse Core Ops, SparseCore 0:
  160.6 155.2 all-reduce.3
where the time goes:
time: 382 us; the launch traced here: 376 us
  waiting for transfers between devices  168 us (44%)
  other arithmetic  77.4 us (20%)
  matrix products  50.2 us (13%)
  local copies, waits for them, and re-layouts  38.7 us (10%)
  starting transfers between devices  26.3 us (7%)
  between operations  14.9 us (4%)
    unnamed x2, waiting for transfers between devices  155 us
    mul x3, other arithmetic, local(): padded = diffuse(padded, depth_view) * mask_view  48.6 us
    dot_general x9, matrix products, matmul_highest(): jnp.dot(left, right, precision=lax.Precision.HIGHEST, preferred_element_t...  40.6 us
    unnamed x28, local copies, waits for them, and re-layouts  26.3 us
    convert_element_type x1, other arithmetic, local(): padded.astype(jnp.bfloat16).reshape(sensors, tile_columns * tile_rows)  21.5 us
    ppermute x4, starting transfers between devices, extended(): lax.ppermute(lax.slice_in_dim(block, block.shape[dim] - width, None, axis...  19.7 us
    ppermute x4, waiting for transfers between devices, extended(): lax.ppermute(lax.slice_in_dim(block, block.shape[dim] - width, None, axis...  12.9 us
    slice x2, local copies, waits for them, and re-layouts, extended(): lax.slice_in_dim(block, block.shape[dim] - width, None, axis=dim)  10.7 us
  transfers between devices with their start and end apart: 9, of which 2 were waited for; matrix products, arithmetic and copies ran while one was open for 8% of the time, Pallas kernels for 0%

commit v1 on v0

--- a/solution.py
+++ b/solution.py
@@ -1,18 +1,18 @@
 import jax
 import jax.numpy as jnp
 from jax import lax
+from jax.experimental import pallas as pl
+from jax.experimental.pallas import tpu as pltpu
 from jax.sharding import PartitionSpec as P
 
 SWEEPS = 4
-ITERS = 4
+MESH = pl.DeviceIdType.MESH
+LANES = 128
+CLASSES = 3
+CLASS_ROWS = 1024
 
 
 diffusion_step = 0.06
-
-
-def over_pieces(shard, axis):
-    pieces = lax.all_gather(shard, axis)
-    return pieces.sum(axis=0)
 
 
 def extended(block, sides, width):
@@ -42,8 +42,154 @@
     return middle + diffusion_step * face_flux
 
 
-def matmul_highest(left, right):
-    return jnp.dot(left, right, precision=lax.Precision.HIGHEST, preferred_element_type=jnp.float32)
+def position():
+    gx, gy = lax.axis_index("gx"), lax.axis_index("gy")
+    x, y, z, core = gy // 4, ((gy // 2) % 2) * 2 + gx // 4, gx % 4, gy % 2
+    return [x, y, z], core
+
+
+def device(place, core):
+    x, y, z = place
+    return ((y % 2) * 4 + z, x * 4 + (y // 2) * 2 + core)
+
+
+def moved(place, axis, step):
+    there = list(place)
+    there[axis] = (place[axis] + step) % 4
+    return there
+
+
+def all_reduce_kernel(part, total, half_in, q_in, e_in, p_in, half, quarter, eighth, send, recv):
+    place, core = position()
+    barrier = pltpu.get_barrier_semaphore()
+    pl.semaphore_signal(barrier, inc=1, device_id=device(place, 1 - core), device_id_type=MESH)
+    for axis in range(3):
+        for step in (1, 2, 3):
+            pl.semaphore_signal(
+                barrier, inc=1, device_id=device(moved(place, axis, step), core), device_id_type=MESH
+            )
+    pl.semaphore_wait(barrier, 10)
+
+    def rows(start, size):
+        return pl.ds(pl.multiple_of(start, 8), size)
+
+    def push(src, dst, sem, place_to, core_to):
+        copy = pltpu.make_async_remote_copy(
+            src_ref=src,
+            dst_ref=dst,
+            send_sem=send.at[sem],
+            recv_sem=recv.at[sem],
+            device_id=device(place_to, core_to),
+            device_id_type=MESH,
+        )
+        copy.start()
+        return copy
+
+    started = []
+    pending = {}
+    for q in range(CLASSES):
+        copy = push(
+            part.at[rows(q * CLASS_ROWS + (1 - core) * 512, 512)],
+            half_in.at[q],
+            q,
+            place,
+            1 - core,
+        )
+        pending[q, 0] = [copy]
+    own = {}
+    sizes = (512, 128, 32, 8)
+    slots = (None, q_in, e_in, p_in)
+    sums = (half, quarter, eighth)
+    base = {q: q * CLASS_ROWS + core * 512 for q in range(CLASSES)}
+    for stage in range(4):
+        for q in range(CLASSES):
+            for copy in pending[q, stage]:
+                copy.wait_recv()
+            started += pending[q, stage]
+            size = sizes[stage]
+            if stage == 0:
+                value = part[rows(base[q], 512), :] + half_in[q]
+            else:
+                axis = (q + stage - 1) % 3
+                value = sums[stage - 1][q, rows(place[axis] * size, size), :]
+                for slot in range(3):
+                    value = value + slots[stage][q, slot]
+                base[q] = base[q] + place[axis] * size
+            if stage == 3:
+                total[rows(base[q], 8), :] = value
+                continue
+            sums[stage][q] = value
+            axis = (q + stage) % 3
+            size = sizes[stage + 1]
+            pending[q, stage + 1] = [
+                push(
+                    sums[stage].at[q, rows(((place[axis] + step) % 4) * size, size)],
+                    slots[stage + 1].at[q, step - 1],
+                    3 + (stage * CLASSES + q) * 3 + step - 1,
+                    moved(place, axis, step),
+                    core,
+                )
+                for step in (1, 2, 3)
+            ]
+    sem0 = 3 + 27
+    for stage in (3, 2, 1, 0):
+        for q in range(CLASSES):
+            if stage < 3:
+                for copy in pending[q, "g", stage + 1]:
+                    copy.wait_recv()
+                started += pending[q, "g", stage + 1]
+                axis = (q + stage) % 3
+                base[q] = base[q] - place[axis] * sizes[stage + 1]
+            size = sizes[stage]
+            here = total.at[rows(base[q], size)]
+            if stage == 0:
+                pending[q, "g", 0] = [push(here, here, sem0 + 27 + q, place, 1 - core)]
+                continue
+            axis = (q + stage - 1) % 3
+            pending[q, "g", stage] = [
+                push(
+                    here,
+                    here,
+                    sem0 + ((stage - 1) * CLASSES + q) * 3 + step - 1,
+                    moved(place, axis, step),
+                    core,
+                )
+                for step in (1, 2, 3)
+            ]
+    for q in range(CLASSES):
+        for copy in pending[q, "g", 0]:
+            copy.wait_recv()
+        started += pending[q, "g", 0]
+    for copy in started:
+        copy.wait_send()
+
+
+def all_reduced(part):
+    vmem = pl.BlockSpec(memory_space=pltpu.VMEM)
+    f32 = jnp.float32
+    return pl.pallas_call(
+        all_reduce_kernel,
+        out_shape=jax.ShapeDtypeStruct(part.shape, f32),
+        in_specs=[vmem],
+        out_specs=vmem,
+        scratch_shapes=[
+            pltpu.VMEM((CLASSES, 512, LANES), f32),
+            pltpu.VMEM((CLASSES, 3, 128, LANES), f32),
+            pltpu.VMEM((CLASSES, 3, 32, LANES), f32),
+            pltpu.VMEM((CLASSES, 3, 8, LANES), f32),
+            pltpu.VMEM((CLASSES, 512, LANES), f32),
+            pltpu.VMEM((CLASSES, 128, LANES), f32),
+            pltpu.VMEM((CLASSES, 32, LANES), f32),
+            pltpu.SemaphoreType.DMA((60,)),
+            pltpu.SemaphoreType.DMA((60,)),
+        ],
+        compiler_params=pltpu.CompilerParams(collective_id=0, has_side_effects=True),
+        name="gram_all_reduce",
+    )(part)
+
+
+def dot3(left, right):
+    return jnp.dot(left, right, precision=lax.Precision.HIGH, preferred_element_type=jnp.float32)
 
 
 def local(adjoint, seafloor_depth, sensor_row, sensor_column, noise_sigma):
@@ -56,9 +202,10 @@
     pick_row = (sensor_row[:, None] - row_offset == jnp.arange(tile_rows)[None, :]).astype(
         jnp.float32
     )
-    picked = jnp.sum(matmul_highest(pick_column, seafloor_depth) * pick_row, axis=1)
-    under_sensor = over_pieces(picked, ("gx", "gy"))
-    variance = noise_sigma * noise_sigma * under_sensor
+    picked = jnp.sum(
+        jnp.dot(pick_column, seafloor_depth, precision=lax.Precision.HIGHEST) * pick_row, axis=1
+    )
+    variance = noise_sigma * noise_sigma * picked
     depth_padded = extended(seafloor_depth, (("gx", 1), ("gy", 0)), SWEEPS)
     inside = (depth_padded > 0.0).astype(jnp.float32)
     padded = extended(adjoint, (("gx", 2), ("gy", 1)), SWEEPS).astype(jnp.float32)
@@ -77,12 +224,22 @@
     partial_value = lax.dot_general(
         smoothed, smoothed, (((1,), (1,)), ((), ())), preferred_element_type=jnp.float32
     )
-    gram = lax.psum(partial_value, ("gx", "gy"))
-    operator = gram * inverse_cells + jnp.diag(variance)
+    partial_value = partial_value * inverse_cells + jnp.diag(variance)
+    blocks = -(-sensors // LANES)
+    wide = jnp.pad(partial_value, ((0, 0), (0, blocks * LANES - sensors)))
+    stacked = jnp.concatenate([wide[:, i * LANES : (i + 1) * LANES] for i in range(blocks)])
+    stacked = jnp.pad(stacked, ((0, CLASSES * CLASS_ROWS - stacked.shape[0]), (0, 0)))
+    stacked = all_reduced(stacked)
+    operator = jnp.concatenate(
+        [stacked[i * sensors : (i + 1) * sensors] for i in range(blocks)], axis=1
+    )[:, :sensors]
     spectral_bound = jnp.max(jnp.sum(jnp.abs(operator), axis=1))
-    inverse = jnp.eye(sensors, dtype=jnp.float32) / spectral_bound
-    for _ in range(ITERS):
-        inverse = 2.0 * inverse - matmul_highest(matmul_highest(inverse, operator), inverse)
+    identity = jnp.eye(sensors, dtype=jnp.float32)
+    residual = identity - operator / spectral_bound
+    inverse = (identity + residual) / spectral_bound
+    for _ in range(3):
+        residual = dot3(residual, residual)
+        inverse = inverse + dot3(residual, inverse)
     gain_field = jnp.dot(inverse.astype(jnp.bfloat16), smoothed, preferred_element_type=jnp.float32)
     return gain_field.astype(jnp.bfloat16).reshape(sensors, tile_columns, tile_rows)
 

time: 382 us -> 225 us (0.59); the launches traced: 376 us -> 224 us
  waiting for transfers between devices: 168 us -> 13 us
  Pallas kernels: 0 us -> 42.4 us
  matrix products: 50.2 us -> 25.2 us
  between operations: 14.9 us -> 0.44 us
    unnamed x2 -> x0, waiting for transfers between devices: 155 us -> none
    pallas_call x0 -> x1, Pallas kernels: none -> 42.4 us  [all_reduced(): pl.pallas_call(all_reduce_kernel, out_shape=jax.ShapeDtypeStruct(part.sha...]
    dot_general x9 -> x7, matrix products: 40.6 us -> 16.8 us  [the longest x6 16.2 us: dot3(): jnp.dot(left, right, precision=lax.Precision.HIGH, preferred_element_type...]
  transfers between devices with their start and end apart: 9 -> 8, of which waited for: 2 -> 1; matrix products, arithmetic and copies ran while one was open for 8% -> 14% of each run, Pallas kernels for 0% -> 0%
where the time goes in v1:
time: 225 us; the launch traced here: 224 us
  other arithmetic  76 us (34%)
  Pallas kernels  42.4 us (19%)
  local copies, waits for them, and re-layouts  41.1 us (18%)
  starting transfers between devices  26.3 us (12%)
  matrix products  25.2 us (11%)
  waiting for transfers between devices  13 us (6%)
    mul x3, other arithmetic, local(): padded = diffuse(padded, depth_view) * mask_view  48.5 us
    pallas_call x1, Pallas kernels, all_reduced(): pl.pallas_call(all_reduce_kernel, out_shape=jax.ShapeDtypeStruct(part.sha...  42.4 us
    unnamed x28, local copies, waits for them, and re-layouts  27.6 us
    convert_element_type x1, other arithmetic, local(): padded.astype(jnp.bfloat16).reshape(sensors, tile_columns * tile_rows)  21.6 us
    ppermute x4, starting transfers between devices, extended(): lax.ppermute(lax.slice_in_dim(block, block.shape[dim] - width, None, axis...  19.7 us
    dot_general x6, matrix products, dot3(): jnp.dot(left, right, precision=lax.Precision.HIGH, preferred_element_type...  16.2 us
    ppermute x4, waiting for transfers between devices, extended(): lax.ppermute(lax.slice_in_dim(block, block.shape[dim] - width, None, axis...  12.9 us
    slice x2, local copies, waits for them, and re-layouts, extended(): lax.slice_in_dim(block, block.shape[dim] - width, None, axis=dim)  10.7 us
  transfers between devices with their start and end apart: 8, of which 1 were waited for; matrix products, arithmetic and copies ran while one was open for 14% of the time, Pallas kernels for 0%

profile of v1, /device:TPU:1, one launch (start us, length us, event | category | flops | bytes accessed | tf_op | source)
XLA Modules:
  0.0 224.4 jit_solution(3378614216642864091)
XLA Ops:
  0.0 0.9 fusion.70
  0.9 4.3 %collective-permute-start.4 = (f32[32,4]{1,0:T(8,128)S(1)}, f32[32,4]{1,0:T(8,128)S(1)}, u32[]{:S(2)}, u32[]{:S(2)}) collective-permute-start(f32[32,4]{1,0:T(8,128)S(1)} %get-tuple-element.31), channel_id=1, source_target_pairs={{0,16},{16,32},{32,48},{48,64},{64,80},{80,96},{96,112},{1,17},{17... | collective-permute-start | bytes 1544 | tf_op jit(solution)/shard_map/ppermute | solution.py:23
  5.2 1.3 collective-permute-start.5
  6.5 9.9 %fusion.69 = (bf16[600,32,4]{2,1,0:T(8,128)(2,1)}, bf16[600,32,4]{2,1,0:T(8,128)(2,1)}) fusion(bf16[600,32,128]{2,1,0:T(8,128)(2,1)} %param.5), kind=kLoop, calls=%fused_computation.136 | loop fusion | bytes 614400 | tf_op jit(solution)/shard_map/slice | solution.py:24
  16.4 5.5 %copy.17 = bf16[600,32,4]{0,1,2:T(8,128)(2,1)S(1)} copy(bf16[600,32,4]{2,1,0:T(8,128)(2,1)} %get-tuple-element.9) | data formatting | bytes 307200
  21.9 4.2 %collective-permute-start = (bf16[600,32,4]{0,1,2:T(8,128)(2,1)S(1)}, bf16[600,32,4]{0,1,2:T(8,128)(2,1)S(1)}, u32[]{:S(2)}, u32[]{:S(2)}) collective-permute-start(bf16[600,32,4]{0,1,2:T(8,128)(2,1)S(1)} %copy.17), channel_id=1, source_target_pairs={{0,16},{16,32},{32,48},{48,64},{64,80},{80,96},{96,112},{1,17},{17... | collective-permute-start | bytes 460808 | tf_op jit(solution)/shard_map/ppermute | solution.py:23
  26.1 5.5 %copy.18 = bf16[600,32,4]{0,1,2:T(8,128)(2,1)S(1)} copy(bf16[600,32,4]{2,1,0:T(8,128)(2,1)} %get-tuple-element.10) | data formatting | bytes 307200
  31.6 1.3 collective-permute-start.1
  32.9 0.0 copy-done.2
  32.9 0.5 fusion.46
  33.5 0.0 collective-permute-done.4
  33.5 0.0 collective-permute-done.5
  33.5 0.1 pad_maximum_fusion.9
  33.6 6.0 %collective-permute-start.6 = (f32[4,136]{1,0:T(4,128)S(1)}, f32[4,136]{1,0:T(4,128)S(1)}, u32[]{:S(2)}, u32[]{:S(2)}) collective-permute-start(f32[4,136]{1,0:T(4,128)S(1)} %get-tuple-element.15), channel_id=1, source_target_pairs={{0,1},{1,2},{2,3},{3,4},{4,5},{5,6},{6,7},{7,8},{8,9},{9,10},{10,1... | collective-permute-start | bytes 6536 | tf_op jit(solution)/shard_map/ppermute | solution.py:23
  39.6 1.9 collective-permute-start.7
  41.6 8.8 %copy.11 = bf16[600,32,128]{0,2,1:T(8,128)(2,1)} copy(bf16[600,32,128]{2,1,0:T(8,128)(2,1)} %param.5) | data formatting | bytes 9830400 | tf_op args[0]
  50.4 0.0 collective-permute-done.6
  50.4 0.0 collective-permute-done.7
  50.4 0.1 compare_convert_fusion
  50.5 0.1 fusion.62
  50.6 0.1 slice.290
  50.7 0.1 slice.301
  50.7 0.1 slice.312
  50.8 0.1 slice.318
  50.9 0.1 pad_maximum_fusion.4
  51.0 0.0 collective-permute-done
  51.0 0.1 copy.10
  51.1 0.0 collective-permute-done.1
  51.1 0.1 copy.12
  51.2 2.1 pad_maximum_fusion.2
  53.3 5.1 %collective-permute-start.2 = (bf16[600,4,136]{0,2,1:T(8,128)(2,1)S(1)}, bf16[600,4,136]{0,2,1:T(8,128)(2,1)S(1)}, u32[]{:S(2)}, u32[]{:S(2)}) collective-permute-start(bf16[600,4,136]{0,2,1:T(8,128)(2,1)S(1)} %get-tuple-element.7), channel_id=1, source_target_pairs={{0,1},{1,2},{2,3},{3,4},{4,5},{5,6},{6,7},{7,8},{8,9},{9,10},{10,1... | collective-permute-start | bytes 1958408 | tf_op jit(solution)/shard_map/ppermute | solution.py:23
  58.5 2.1 collective-permute-start.3
  60.6 0.1 fusion.64
  60.7 0.1 fusion.58
  60.8 0.1 fusion.54
  60.9 12.9 %collective-permute-done.2 = bf16[600,4,136]{0,2,1:T(8,128)(2,1)S(1)} collective-permute-done((bf16[600,4,136]{0,2,1:T(8,128)(2,1)S(1)}, bf16[600,4,136]{0,2,1:T(8,128)(2,1)S(1)}, u32[]{:S(2)}, u32[]{:S(2)}) %collective-permute-start.2) | collective-permute-done | bytes 652832 | tf_op jit(solution)/shard_map/ppermute | solution.py:23
  73.9 0.0 collective-permute-done.3
  73.9 2.2 %maximum_convert_fusion = f32[600,40,136]{0,2,1:T(8,128)S(1)} fusion(bf16[600,4,136]{0,2,1:T(8,128)(2,1)S(1)} %collective-permute-done.3, bf16[600,32,4]{0,2,1:T(4,128)(2,1)S(1)} %copy.12, bf16[600,32,128]{0,2,1:T(8,128)(2,1)S(1)} %copy-done, bf16[600,32,4]{0,2,1:T(4,128)(2,1)S(1)} %copy.10, bf16[600,4,136]{0,2,1:T(8,128)(2,1)S(1)} %collective-permute-done.2), kind=kLoop, calls=%fused_computation.57 | loop fusion | flops 32640000 | bytes 19584000 | tf_op jit(solution)/shard_map/convert_element_type | solution.py:211
  76.1 12.2 %fusion.4 = f32[600,38,134]{0,2,1:T(8,128)} fusion(f32[600,40,136]{0,2,1:T(8,128)S(1)} %maximum_convert_fusion, f32[38,134]{1,0:T(8,128)S(1)} %slice.290, f32[38,134]{1,0:T(8,128)S(1)} %get-tuple-element.26, f32[38,134]{1,0:T(8,128)S(1)} %get-tuple-element.27, f32[38,134]{1,0:T(8,128)S(1)} %get-tuple-element.28, f32[38,134]{1,0:T(8,128)S(1)} %get-tuple-element.25), kind=kLoop, calls=%fused_computation.5 | loop fusion | flops 42772800 | bytes 73426640 | tf_op jit(solution)/shard_map/mul | solution.py:221
  88.3 25.5 %fusion.14 = f32[600,36,132]{0,2,1:T(8,128)S(1)} fusion(f32[600,38,134]{0,2,1:T(8,128)} %fusion.4, f32[36,132]{1,0:T(8,128)S(1)} %slice.301, f32[36,132]{1,0:T(8,128)S(1)} %get-tuple-element.22, f32[36,132]{1,0:T(8,128)S(1)} %get-tuple-element.23, f32[36,132]{1,0:T(8,128)S(1)} %get-tuple-element.24, f32[36,132]{1,0:T(8,128)S(1)} %get-tuple-element.21), kind=kLoop, calls=%fused_computation.19 | loop fusion | flops 39916800 | bytes 68523840 | tf_op jit(solution)/shard_map/mul | solution.py:221
  113.9 10.8 %fusion.24 = f32[600,34,130]{0,2,1:T(8,128)} fusion(f32[600,36,132]{0,2,1:T(8,128)S(1)} %fusion.14, f32[34,130]{1,0:T(8,128)S(1)} %slice.312, f32[34,130]{1,0:T(8,128)S(1)} %get-tuple-element.19, f32[34,130]{1,0:T(8,128)S(1)} %get-tuple-element.18, f32[34,130]{1,0:T(8,128)S(1)} %get-tuple-element.20, f32[34,130]{1,0:T(8,128)S(1)} %get-tuple-element.17), kind=kLoop, calls=%fused_computation.33 | loop fusion | flops 37128000 | bytes 63736400 | tf_op jit(solution)/shard_map/mul | solution.py:221
  124.6 21.6 %fusion.35 = bf16[600,32,128]{0,2,1:T(8,128)(2,1)S(1)} fusion(f32[600,34,130]{0,2,1:T(8,128)} %fusion.24, f32[32,128]{1,0:T(8,128)S(1)} %slice.318, f32[32,128]{1,0:T(8,128)S(1)} %get-tuple-element.12, f32[32,128]{1,0:T(8,128)S(1)} %get-tuple-element.11, f32[32,128]{1,0:T(8,128)S(1)} %get-tuple-element.30, f32[32,128]{1,0:T(8,128)S(1)} %get-tuple-element.29), kind=kLoop, calls=%fused_computation.48 | loop fusion | flops 36864000 | bytes 54149120 | tf_op jit(solution)/shard_map/convert_element_type | solution.py:222
  146.2 0.0 copy-start.1
  146.3 4.1 %fusion.44 = f32[600,600]{1,0:T(8,128)S(1)} fusion(bf16[600,32,128]{0,2,1:T(8,128)(2,1)S(1)} %fusion.35, f32[600]{0:T(1024)S(1)} %multiply_multiply_fusion), kind=kOutput, calls=%fused_computation.67 | convolution fusion | flops 2950559744 | bytes 6357600 | tf_op jit(solution)/shard_map/dot_general | solution.py:224
  150.6 1.2 pad.9.part
  151.8 42.4 %gram_all_reduce.1 = f32[3072,128]{1,0:T(8,128)} custom-call(f32[3072,128]{1,0:T(8,128)} %pad.9.part), custom_call_target="tpu_custom_call" | custom-call | tf_op jit(solution)/shard_map/gram_all_reduce/pallas_call | solution.py:170
  194.2 1.0 slice_dynamic-update-slice_fusion.8
  195.2 1.0 slice_dynamic-update-slice_fusion.7
  196.2 1.0 slice_dynamic-update-slice_fusion.6
  197.2 1.0 slice_dynamic-update-slice_fusion.5
  198.2 1.0 slice_dynamic-update-slice_fusion.4
  199.1 0.2 abs_reduce_fusion
  199.4 0.6 reduce_max.9
  200.0 3.1 %fusion.48 = f32[600,600]{1,0:T(8,128)S(1)} fusion(f32[600,640]{1,0:T(8,128)S(1)} %slice_dynamic-update-slice_fusion.4, f32[]{:T(128)} %reduce_max.9), kind=kOutput, calls=%fused_computation.78 | convolution fusion | flops 1297440000 | bytes 2976004 | tf_op jit(solution)/shard_map/dot_general | solution.py:192
  203.1 3.1 %convolution_add_fusion.2 = f32[600,600]{1,0:T(8,128)S(1)} fusion(f32[600,600]{1,0:T(8,128)S(1)} %fusion.48, f32[]{:T(128)} %reduce_max.9, f32[600,640]{1,0:T(8,128)S(1)} %slice_dynamic-update-slice_fusion.4), kind=kOutput, calls=%fused_computation.64 | convolution fusion | flops 1298520064 | bytes 4416004 | tf_op jit(solution)/shard_map/dot_general | solution.py:192
  206.2 2.7 %fusion.71 = f32[600,600]{1,0:T(8,128)S(1)} fusion(f32[600,600]{1,0:T(8,128)S(1)} %fusion.48), kind=kOutput, calls=%fused_computation.138 | convolution fusion | flops 1296000000 | bytes 2880000 | tf_op jit(solution)/shard_map/dot_general | solution.py:192
  208.9 0.0 slice-start
  208.9 2.4 %fusion.72 = f32[600,600]{1,0:T(8,128)S(1)} fusion(f32[600,600]{1,0:T(8,128)S(1)} %fusion.71), kind=kOutput, calls=%fused_computation.139 | convolution fusion | flops 1296000000 | bytes 2880000 | tf_op jit(solution)/shard_map/dot_general | solution.py:192
  211.3 0.0 slice-start.1
  211.3 2.5 %convolution_add_fusion.1 = f32[600,600]{1,0:T(8,128)S(1)} fusion(f32[600,600]{1,0:T(8,128)S(1)} %convolution_add_fusion.2, f32[600,600]{1,0:T(8,128)S(1)} %fusion.71), kind=kOutput, calls=%fused_computation.63 | convolution fusion | flops 1296359936 | bytes 4320000 | tf_op jit(solution)/shard_map/dot_general | solution.py:192
  213.8 2.4 %fusion.45 = bf16[600,600]{1,0:T(8,128)(2,1)S(1)} fusion(f32[600,600]{1,0:T(8,128)S(1)} %convolution_add_fusion.1, f32[600,600]{1,0:T(8,128)S(1)} %fusion.72), kind=kOutput, calls=%fused_computation.71 | convolution fusion | flops 1296720000 | bytes 3600000 | tf_op jit(solution)/shard_map/dot_general | solution.py:192
  216.3 0.0 slice-done
  216.3 4.3 %fusion.41 = bf16[75,8,32,128]{3,1,2,0:T(8,128)(2,1)S(1)} fusion(bf16[600,600]{1,0:T(8,128)(2,1)S(1)} %fusion.45, bf16[600,4096]{0,1:T(8,128)(2,1)S(1)} %bitcast.24), kind=kOutput, calls=%fused_computation.59 | convolution fusion | flops 2951577600 | bytes 10550400 | tf_op jit(solution)/shard_map/dot_general | solution.py:243
  220.6 3.8 %copy.19 = bf16[75,8,32,128]{3,2,1,0:T(8,128)(2,1)} copy(bf16[75,8,32,128]{3,1,2,0:T(8,128)(2,1)S(1)} %fusion.41) | data formatting | bytes 9830400
  (19 shorter events, 0.1 us)
Async XLA Ops:
  0.9 32.6 %collective-permute-start.4 = (f32[32,4]{1,0:T(8,128)S(1)}, f32[32,4]{1,0:T(8,128)S(1)}, u32[]{:S(2)}, u32[]{:S(2)}) collective-permute-start(f32[32,4]{1,0:T(8,128)S(1)} %get-tuple-element.31), channel_id=1, source_target_pairs={{0,16},{16,32},{32,48},{48,64},{64,80},{80,96},{96,112},{1,17},{17... | collective-permute-start | bytes 1544 | tf_op jit(solution)/shard_map/ppermute | solution.py:23
  5.2 28.3 %collective-permute-start.5 = (f32[32,4]{1,0:T(8,128)S(1)}, f32[32,4]{1,0:T(8,128)S(1)}, u32[]{:S(2)}, u32[]{:S(2)}) collective-permute-start(f32[32,4]{1,0:T(8,128)S(1)} %get-tuple-element.32), channel_id=1, source_target_pairs={{16,0},{32,16},{48,32},{64,48},{80,64},{96,80},{112,96},{17,1},{33... | collective-permute-start | bytes 1544 | tf_op jit(solution)/shard_map/ppermute | solution.py:26
  16.4 16.5 %copy-start.3 = (s32[600]{0:T(1024)S(1)}, s32[600]{0:T(1024)}, u32[]{:S(2)}) copy-start(s32[600]{0:T(1024)} %param.8) | copy-start | bytes 7204
  16.4 16.5 %copy-start.4 = (s32[600]{0:T(1024)S(1)}, s32[600]{0:T(1024)}, u32[]{:S(2)}) copy-start(s32[600]{0:T(1024)} %param.7) | copy-start | bytes 7204
  16.4 16.5 %copy-start.2 = (f32[32,128]{1,0:T(8,128)S(1)}, f32[32,128]{1,0:T(8,128)}, u32[]{:S(2)}) copy-start(f32[32,128]{1,0:T(8,128)} %param.6) | copy-start | bytes 49156
  16.4 25.1 %copy-start.5 = (f32[600]{0:T(1024)S(1)}, f32[600]{0:T(1024)}, u32[]{:S(2)}) copy-start(f32[600]{0:T(1024)} %param.9) | copy-start | bytes 7204
  21.9 29.1 %collective-permute-start = (bf16[600,32,4]{0,1,2:T(8,128)(2,1)S(1)}, bf16[600,32,4]{0,1,2:T(8,128)(2,1)S(1)}, u32[]{:S(2)}, u32[]{:S(2)}) collective-permute-start(bf16[600,32,4]{0,1,2:T(8,128)(2,1)S(1)} %copy.17), channel_id=1, source_target_pairs={{0,16},{16,32},{32,48},{48,64},{64,80},{80,96},{96,112},{1,17},{17... | collective-permute-start | bytes 460808 | tf_op jit(solution)/shard_map/ppermute | solution.py:23
  31.6 19.5 %collective-permute-start.1 = (bf16[600,32,4]{0,1,2:T(8,128)(2,1)S(1)}, bf16[600,32,4]{0,1,2:T(8,128)(2,1)S(1)}, u32[]{:S(2)}, u32[]{:S(2)}) collective-permute-start(bf16[600,32,4]{0,1,2:T(8,128)(2,1)S(1)} %copy.18), channel_id=1, source_target_pairs={{16,0},{32,16},{48,32},{64,48},{80,64},{96,80},{112,96},{17,1},{33... | collective-permute-start | bytes 460808 | tf_op jit(solution)/shard_map/ppermute | solution.py:26
  33.6 16.8 %collective-permute-start.6 = (f32[4,136]{1,0:T(4,128)S(1)}, f32[4,136]{1,0:T(4,128)S(1)}, u32[]{:S(2)}, u32[]{:S(2)}) collective-permute-start(f32[4,136]{1,0:T(4,128)S(1)} %get-tuple-element.15), channel_id=1, source_target_pairs={{0,1},{1,2},{2,3},{3,4},{4,5},{5,6},{6,7},{7,8},{8,9},{9,10},{10,1... | collective-permute-start | bytes 6536 | tf_op jit(solution)/shard_map/ppermute | solution.py:23
  39.6 10.8 %collective-permute-start.7 = (f32[4,136]{1,0:T(4,128)S(1)}, f32[4,136]{1,0:T(4,128)S(1)}, u32[]{:S(2)}, u32[]{:S(2)}) collective-permute-start(f32[4,136]{1,0:T(4,128)S(1)} %get-tuple-element.16), channel_id=1, source_target_pairs={{1,0},{2,1},{3,2},{4,3},{5,4},{6,5},{7,6},{8,7},{9,8},{10,9},{11,1... | collective-permute-start | bytes 6536 | tf_op jit(solution)/shard_map/ppermute | solution.py:26
  50.4 23.5 %copy-start = (bf16[600,32,128]{0,2,1:T(8,128)(2,1)S(1)}, bf16[600,32,128]{0,2,1:T(8,128)(2,1)}, u32[]{:S(2)}) copy-start(bf16[600,32,128]{0,2,1:T(8,128)(2,1)} %copy.11) | copy-start | bytes 14745604
  53.3 20.6 %collective-permute-start.2 = (bf16[600,4,136]{0,2,1:T(8,128)(2,1)S(1)}, bf16[600,4,136]{0,2,1:T(8,128)(2,1)S(1)}, u32[]{:S(2)}, u32[]{:S(2)}) collective-permute-start(bf16[600,4,136]{0,2,1:T(8,128)(2,1)S(1)} %get-tuple-element.7), channel_id=1, source_target_pairs={{0,1},{1,2},{2,3},{3,4},{4,5},{5,6},{6,7},{7,8},{8,9},{9,10},{10,1... | collective-permute-start | bytes 1958408 | tf_op jit(solution)/shard_map/ppermute | solution.py:23
  58.5 15.4 %collective-permute-start.3 = (bf16[600,4,136]{0,2,1:T(8,128)(2,1)S(1)}, bf16[600,4,136]{0,2,1:T(8,128)(2,1)S(1)}, u32[]{:S(2)}, u32[]{:S(2)}) collective-permute-start(bf16[600,4,136]{0,2,1:T(8,128)(2,1)S(1)} %get-tuple-element.8), channel_id=1, source_target_pairs={{1,0},{2,1},{3,2},{4,3},{5,4},{6,5},{7,6},{8,7},{9,8},{10,9},{11,1... | collective-permute-start | bytes 1958408 | tf_op jit(solution)/shard_map/ppermute | solution.py:26
  146.2 4.2 %copy-start.1 = (bf16[600,32,128]{0,2,1:T(8,128)(2,1)}, bf16[600,32,128]{0,2,1:T(8,128)(2,1)S(1)}, u32[]{:S(2)}) copy-start(bf16[600,32,128]{0,2,1:T(8,128)(2,1)S(1)} %fusion.35) | copy-start | bytes 14745604
  208.9 7.4 %slice-start = ((s8[5242880]{0:T(1024)(128)(4,1)}), s8[4194304]{0:T(1024)(128)(4,1)S(1)}, s32[]{:S(2)}) async-start(s8[5242880]{0:T(1024)(128)(4,1)} %bitcast.22), calls=%async_computation | async-start | bytes 8388608
  211.3 5.0 %slice-start.1 = ((s8[5242880]{0:T(1024)(128)(4,1)}), s8[1048576]{0:T(1024)(128)(4,1)S(1)}, s32[]{:S(2)}) async-start(s8[5242880]{0:T(1024)(128)(4,1)} %bitcast.22), calls=%async_computation.1 | async-start | bytes 2097152

commit v2 on v1

--- a/solution.py
+++ b/solution.py
@@ -13,33 +13,6 @@
 
 
 diffusion_step = 0.06
-
-
-def extended(block, sides, width):
-    for axis, dim in sides:
-        count = lax.axis_size(axis)
-        forward = [(i, i + 1) for i in range(count - 1)]
-        backward = [(target, source) for source, target in forward]
-        low = lax.ppermute(
-            lax.slice_in_dim(block, block.shape[dim] - width, None, axis=dim), axis, forward
-        )
-        high = lax.ppermute(lax.slice_in_dim(block, 0, width, axis=dim), axis, backward)
-        block = jnp.concatenate([low, block, high], axis=dim)
-    return block
-
-
-def diffuse(padded, depth_padded):
-    centre = depth_padded[1:-1, 1:-1]
-    north_face = 0.5 * (centre + depth_padded[1:-1, 2:])
-    south_face = 0.5 * (centre + depth_padded[1:-1, :-2])
-    east_face = 0.5 * (centre + depth_padded[2:, 1:-1])
-    west_face = 0.5 * (centre + depth_padded[:-2, 1:-1])
-    middle = padded[:, 1:-1, 1:-1]
-    face_flux = north_face * (padded[:, 1:-1, 2:] - middle)
-    face_flux = face_flux + south_face * (padded[:, 1:-1, :-2] - middle)
-    face_flux = face_flux + east_face * (padded[:, 2:, 1:-1] - middle)
-    face_flux = face_flux + west_face * (padded[:, :-2, 1:-1] - middle)
-    return middle + diffusion_step * face_flux
 
 
 def position():
@@ -192,6 +165,269 @@
     return jnp.dot(left, right, precision=lax.Precision.HIGH, preferred_element_type=jnp.float32)
 
 
+SENSORS = 600
+WIDE = 640
+CHUNKS = WIDE // LANES
+TOP = 16
+BLOCK = 48
+DIRECTIONS = ((0, 1), (0, -1), (1, 0), (-1, 0), (1, 1), (1, -1), (-1, 1), (-1, -1))
+
+
+def smooth_kernel(
+    field, depth, variance, smoothed, gram,
+    level0, coefficient, levels, total, west, east, low_rows, high_rows, low_send, high_send,
+    depths, send, recv,
+):
+    gx, gy = lax.axis_index("gx"), lax.axis_index("gy")
+    columns, rows, _ = field.shape
+    f32, bf16 = jnp.float32, jnp.bfloat16
+
+    def neighbour(step):
+        return (lax.rem(gx + step[0] + 8, 8), lax.rem(gy + step[1] + 16, 16))
+
+    barrier = pltpu.get_barrier_semaphore()
+    for step in DIRECTIONS:
+        pl.semaphore_signal(barrier, inc=1, device_id=neighbour(step), device_id_type=MESH)
+
+    upper = lax.broadcasted_iota(jnp.int32, (8, WIDE), 0) < 4
+
+    def pack(group, _):
+        first, last = [], []
+        for pair in (0, 1):
+            at = group * 4 + pair * 2
+            a = field[at, pl.ds(0, 16), :].astype(f32)[:8]
+            b = field[at + 1, pl.ds(0, 16), :].astype(f32)[:8]
+            first.append(jnp.where(upper, a, pltpu.roll(b, 4, 0)))
+            a = field[at, pl.ds(rows - 16, 16), :].astype(f32)[8:]
+            b = field[at + 1, pl.ds(rows - 16, 16), :].astype(f32)[8:]
+            last.append(jnp.where(upper, pltpu.roll(a, 4, 0), b))
+        at = pl.ds(pl.multiple_of(group * 16, 16), 16)
+        low_send[at, :] = jnp.concatenate(first).astype(bf16)
+        high_send[at, :] = jnp.concatenate(last).astype(bf16)
+        return 0
+
+    lax.fori_loop(0, columns // 4, pack, 0)
+    pl.semaphore_wait(barrier, 8)
+
+    def push(src, dst, sem, step):
+        copy = pltpu.make_async_remote_copy(
+            src_ref=src,
+            dst_ref=dst,
+            send_sem=send.at[sem],
+            recv_sem=recv.at[sem],
+            device_id=neighbour(step),
+            device_id_type=MESH,
+        )
+        copy.start()
+        return copy
+
+    n4 = columns * 4
+    depth_copies = [push(depth, depths.at[k], k, DIRECTIONS[k]) for k in range(8)]
+    halo_copies = [
+        push(field.at[pl.ds(columns - 4, 4)], west, 8, (0, 1)),
+        push(field.at[pl.ds(0, 4)], east, 9, (0, -1)),
+        push(high_send, low_rows.at[pl.ds(16, n4)], 10, (1, 0)),
+        push(low_send, high_rows.at[pl.ds(16, n4)], 11, (-1, 0)),
+        push(high_send.at[pl.ds(n4 - 16, 16)], low_rows.at[pl.ds(0, 16)], 12, (1, 1)),
+        push(high_send.at[pl.ds(0, 16)], low_rows.at[pl.ds(n4 + 16, 16)], 13, (1, -1)),
+        push(low_send.at[pl.ds(n4 - 16, 16)], high_rows.at[pl.ds(0, 16)], 14, (-1, 1)),
+        push(low_send.at[pl.ds(0, 16)], high_rows.at[pl.ds(n4 + 16, 16)], 15, (-1, -1)),
+    ]
+
+    def widen(src, at, to):
+        for chunk in range(CHUNKS):
+            level0[to, chunk, pl.ds(TOP, rows), :] = src[
+                at, :, pl.ds(chunk * LANES, LANES)
+            ].astype(f32)
+
+    def fill(column, _):
+        widen(field, column, column + 4)
+        return 0
+
+    lax.fori_loop(0, columns, fill, 0)
+
+    for copy in depth_copies:
+        copy.wait_recv()
+    inside_x = {1: gx > 0, -1: gx < 7, 0: gx >= 0}
+    inside_y = {1: gy > 0, -1: gy < 15, 0: gy >= 0}
+
+    def tile(step):
+        if step == (0, 0):
+            return depth[...]
+        keep = jnp.logical_and(inside_x[step[0]], inside_y[step[1]])
+        return depths[DIRECTIONS.index(step)] * jnp.where(keep, 1.0, 0.0)
+
+    turned = []
+    for dx in (1, 0, -1):
+        stack = jnp.concatenate(
+            [
+                tile((dx, 1))[columns - 8 :],
+                tile((dx, 0)),
+                tile((dx, -1))[:8],
+                jnp.zeros((LANES - columns - 16, rows), f32),
+            ]
+        )
+        turned.append(jnp.transpose(stack))
+    here = jnp.concatenate([turned[0][rows - TOP :], turned[1], turned[2][:TOP]])
+    height = rows + 2 * TOP
+    others = (
+        pltpu.roll(here, height - 1, 0),
+        pltpu.roll(here, 1, 0),
+        pltpu.roll(here, LANES - 1, 1),
+        pltpu.roll(here, 1, 1),
+    )
+    weights = [diffusion_step * (0.5 * (here + other)) for other in others]
+    kept = [jnp.where(other > 0.0, w, 0.0) for other, w in zip(others, weights)]
+    centre = 1.0 - (weights[0] + weights[1] + weights[2] + weights[3])
+    for index, value in enumerate([centre] + kept):
+        value = value[8 : height - 8]
+        for column in range(columns + 6):
+            coefficient[index, column] = jnp.broadcast_to(
+                value[:, column + 5 : column + 6], (height - 16, LANES)
+            )
+
+    for copy in halo_copies:
+        copy.wait_recv()
+
+    def edge(column, _):
+        widen(west, column, column)
+        widen(east, column, column + columns + 4)
+        return 0
+
+    lax.fori_loop(0, 4, edge, 0)
+
+    def rims(group, _):
+        at = pl.ds(pl.multiple_of(group * 16, 16), 16)
+        low, high = low_rows[at, :].astype(f32), high_rows[at, :].astype(f32)
+        for pair in (0, 1):
+            for odd in (0, 1):
+                a, b = low[pair * 8 : pair * 8 + 8], high[pair * 8 : pair * 8 + 8]
+                if odd:
+                    b = pltpu.roll(b, 4, 0)
+                else:
+                    a = pltpu.roll(a, 4, 0)
+                for chunk in range(CHUNKS):
+                    part = slice(chunk * LANES, (chunk + 1) * LANES)
+                    column = group * 4 + pair * 2 + odd
+                    level0[column, chunk, pl.ds(TOP - 8, 8), :] = a[:, part]
+                    level0[column, chunk, pl.ds(TOP + rows, 8), :] = b[:, part]
+        return 0
+
+    lax.fori_loop(0, (columns + 8) // 4, rims, 0)
+
+    def sweep(read, write, column, first, last):
+        for start in range(first, last, BLOCK):
+            size = min(BLOCK, last - start)
+            k = [coefficient[index, column, pl.ds(8 + start, size), :] for index in range(5)]
+            for chunk in range(CHUNKS):
+                at = TOP + start
+                write(
+                    chunk,
+                    start,
+                    size,
+                    k[0] * read(1, chunk, at, size)
+                    + k[1] * read(1, chunk, at + 1, size)
+                    + k[2] * read(1, chunk, at - 1, size)
+                    + k[3] * read(2, chunk, at, size)
+                    + k[4] * read(0, chunk, at, size),
+                )
+
+    def wave(i, _):
+        slots = [lax.rem(i + 1, 3), lax.rem(i + 2, 3), lax.rem(i, 3)]
+
+        def read_first(which, chunk, at, size):
+            return level0[i + which, chunk, pl.ds(at, size), :]
+
+        def read_level(level):
+            return lambda which, chunk, at, size: levels[
+                level, slots[which], chunk, pl.ds(at, size), :
+            ]
+
+        def write_level(level):
+            def write(chunk, start, size, value):
+                levels[level, slots[2], chunk, pl.ds(TOP + start, size), :] = value
+
+            return write
+
+        sweep(read_first, write_level(0), i, -8, rows + 8)
+        sweep(read_level(0), write_level(1), jnp.maximum(i - 1, 0), -8, rows + 8)
+        sweep(read_level(1), write_level(2), jnp.maximum(i - 2, 0), -8, rows + 8)
+
+        @pl.when(i >= 6)
+        def _():
+            def write(chunk, start, size, value):
+                smoothed[i - 6, pl.ds(start, size), pl.ds(chunk * LANES, LANES)] = value.astype(
+                    bf16
+                )
+
+            sweep(read_level(2), write, i - 3, 0, rows)
+
+        return 0
+
+    lax.fori_loop(0, columns + 6, wave, 0)
+
+    total[...] = jnp.zeros_like(total)
+
+    def accumulate(group, _):
+        part = smoothed[pl.ds(group * 8, 8)].reshape(8 * rows, WIDE)
+        total[...] += lax.dot_general(
+            part, part, (((0,), (0,)), ((), ())), preferred_element_type=f32
+        )
+        return 0
+
+    lax.fori_loop(0, columns // 8, accumulate, 0)
+    sensors = SENSORS
+    inverse_cells = 1.0 / (columns * rows * 128)
+    for chunk in range(CHUNKS):
+        part = slice(chunk * LANES, (chunk + 1) * LANES)
+        row = lax.broadcasted_iota(jnp.int32, (sensors, LANES), 0)
+        lane = lax.broadcasted_iota(jnp.int32, (sensors, LANES), 1) + chunk * LANES
+        gram[pl.ds(chunk * sensors, sensors), :] = total[:sensors, part] * inverse_cells + jnp.where(
+            row == lane, variance[:, part], 0.0
+        )
+    gram[pl.ds(CHUNKS * sensors, gram.shape[0] - CHUNKS * sensors), :] = jnp.zeros(
+        (gram.shape[0] - CHUNKS * sensors, LANES), f32
+    )
+    for copy in depth_copies + halo_copies:
+        copy.wait_send()
+
+
+def smoothed_and_gram(field, depth, variance):
+    vmem = pl.BlockSpec(memory_space=pltpu.VMEM)
+    f32, bf16 = jnp.float32, jnp.bfloat16
+    columns, rows, _ = field.shape
+    height = rows + 2 * TOP
+    rim = pltpu.VMEM(((columns + 8) * 4, WIDE), bf16)
+    return pl.pallas_call(
+        smooth_kernel,
+        out_shape=(
+            jax.ShapeDtypeStruct(field.shape, bf16),
+            jax.ShapeDtypeStruct((CLASSES * CLASS_ROWS, LANES), f32),
+        ),
+        in_specs=[vmem] * 3,
+        out_specs=(vmem, vmem),
+        scratch_shapes=[
+            pltpu.VMEM((columns + 8, CHUNKS, height, LANES), f32),
+            pltpu.VMEM((5, columns + 6, height - 16, LANES), f32),
+            pltpu.VMEM((3, 3, CHUNKS, height, LANES), f32),
+            pltpu.VMEM((WIDE, WIDE), f32),
+            pltpu.VMEM((4, rows, WIDE), bf16),
+            pltpu.VMEM((4, rows, WIDE), bf16),
+            rim,
+            rim,
+            pltpu.VMEM((columns * 4, WIDE), bf16),
+            pltpu.VMEM((columns * 4, WIDE), bf16),
+            pltpu.VMEM((8, columns, rows), f32),
+            pltpu.SemaphoreType.DMA((16,)),
+            pltpu.SemaphoreType.DMA((16,)),
+        ],
+        compiler_params=pltpu.CompilerParams(
+            collective_id=1, has_side_effects=True, vmem_limit_bytes=66_000_000
+        ),
+        name="smooth_and_gram",
+    )(field, depth, variance)
+
+
 def local(adjoint, seafloor_depth, sensor_row, sensor_column, noise_sigma):
     sensors, tile_columns, tile_rows = adjoint.shape
     column_offset = lax.axis_index("gy") * tile_columns
@@ -206,32 +442,12 @@
         jnp.dot(pick_column, seafloor_depth, precision=lax.Precision.HIGHEST) * pick_row, axis=1
     )
     variance = noise_sigma * noise_sigma * picked
-    depth_padded = extended(seafloor_depth, (("gx", 1), ("gy", 0)), SWEEPS)
-    inside = (depth_padded > 0.0).astype(jnp.float32)
-    padded = extended(adjoint, (("gx", 2), ("gy", 1)), SWEEPS).astype(jnp.float32)
-    padded_columns, padded_rows = depth_padded.shape
-    for sweep_index in range(SWEEPS):
-        depth_view = depth_padded[
-            sweep_index : padded_columns - sweep_index, sweep_index : padded_rows - sweep_index
-        ]
-        mask_view = inside[
-            sweep_index + 1 : padded_columns - sweep_index - 1,
-            sweep_index + 1 : padded_rows - sweep_index - 1,
-        ]
-        padded = diffuse(padded, depth_view) * mask_view
-    smoothed = padded.astype(jnp.bfloat16).reshape(sensors, tile_columns * tile_rows)
-    inverse_cells = 1.0 / (tile_columns * tile_rows * lax.axis_size("gx") * lax.axis_size("gy"))
-    partial_value = lax.dot_general(
-        smoothed, smoothed, (((1,), (1,)), ((), ())), preferred_element_type=jnp.float32
-    )
-    partial_value = partial_value * inverse_cells + jnp.diag(variance)
-    blocks = -(-sensors // LANES)
-    wide = jnp.pad(partial_value, ((0, 0), (0, blocks * LANES - sensors)))
-    stacked = jnp.concatenate([wide[:, i * LANES : (i + 1) * LANES] for i in range(blocks)])
-    stacked = jnp.pad(stacked, ((0, CLASSES * CLASS_ROWS - stacked.shape[0]), (0, 0)))
+    variance = jnp.pad(variance, (0, WIDE - sensors)).reshape(1, WIDE)
+    field = jnp.pad(jnp.transpose(adjoint, (1, 2, 0)), ((0, 0), (0, 0), (0, WIDE - sensors)))
+    smoothed, stacked = smoothed_and_gram(field, seafloor_depth, variance)
     stacked = all_reduced(stacked)
     operator = jnp.concatenate(
-        [stacked[i * sensors : (i + 1) * sensors] for i in range(blocks)], axis=1
+        [stacked[i * sensors : (i + 1) * sensors] for i in range(CHUNKS)], axis=1
     )[:, :sensors]
     spectral_bound = jnp.max(jnp.sum(jnp.abs(operator), axis=1))
     identity = jnp.eye(sensors, dtype=jnp.float32)
@@ -240,8 +456,11 @@
     for _ in range(3):
         residual = dot3(residual, residual)
         inverse = inverse + dot3(residual, inverse)
-    gain_field = jnp.dot(inverse.astype(jnp.bfloat16), smoothed, preferred_element_type=jnp.float32)
-    return gain_field.astype(jnp.bfloat16).reshape(sensors, tile_columns, tile_rows)
+    inverse = jnp.pad(inverse.astype(jnp.bfloat16), ((0, 0), (0, WIDE - sensors)))
+    gain_field = lax.dot_general(
+        inverse, smoothed, (((1,), (2,)), ((), ())), preferred_element_type=jnp.float32
+    )
+    return gain_field.astype(jnp.bfloat16)
 
 
 def solution(mesh):

time: 225 us -> 144 us (0.64)
  other arithmetic: 76 us -> 2.21 us
  Pallas kernels: 42.4 us -> 96.1 us
  starting transfers between devices: 26.3 us -> 0 us
  local copies, waits for them, and re-layouts: 41.1 us -> 23.2 us
  waiting for transfers between devices: 13 us -> 0 us
  matrix products: 25.2 us -> 21.7 us
    pallas_call x0 -> x1, Pallas kernels: none -> 59.5 us  [smoothed_and_gram(): pl.pallas_call(smooth_kernel, out_shape=(jax.ShapeDtypeStruct(field.shape...]
    mul x7 -> x0, other arithmetic: 48.9 us -> none  [the longest x3 48.5 us: local(): padded = diffuse(padded, depth_view) * mask_view]
    ppermute x8 -> x0, starting transfers between devices: 26.3 us -> none  [the longest x4 19.7 us: extended(): lax.ppermute(lax.slice_in_dim(block, block.shape[dim] - width, None, axis...]
    convert_element_type x3 -> x0, other arithmetic: 24 us -> none  [the longest x1 21.6 us: local(): padded.astype(jnp.bfloat16).reshape(sensors, tile_columns * tile_rows)]
    unnamed x28 -> x9, local copies, waits for them, and re-layouts: 27.6 us -> 12.9 us
    ppermute x8 -> x0, waiting for transfers between devices: 13 us -> none  [the longest x4 12.9 us: extended(): lax.ppermute(lax.slice_in_dim(block, block.shape[dim] - width, None, axis...]
    slice x6 -> x0, local copies, waits for them, and re-layouts: 11 us -> none  [the longest x2 10.7 us: extended(): lax.slice_in_dim(block, block.shape[dim] - width, None, axis=dim)]
    pallas_call x1, Pallas kernels: 42.4 us -> 36.6 us  [all_reduced(): pl.pallas_call(all_reduce_kernel, out_shape=jax.ShapeDtypeStruct(part.sha...]
  transfers between devices with their start and end apart: 8 -> 0, of which waited for: 1 -> 0; matrix products, arithmetic and copies ran while one was open for 14% -> 0% of each run, Pallas kernels for 0% -> 0%
where the time goes in v2:
time: 144 us; the launch traced here: 143 us
  Pallas kernels  96.1 us (67%)
  local copies, waits for them, and re-layouts  23.2 us (16%)
  matrix products  21.7 us (15%)
  other arithmetic  2.21 us (2%)
    pallas_call x1, Pallas kernels, smoothed_and_gram(): pl.pallas_call(smooth_kernel, out_shape=(jax.ShapeDtypeStruct(field.shape...  59.5 us
    pallas_call x1, Pallas kernels, all_reduced(): pl.pallas_call(all_reduce_kernel, out_shape=jax.ShapeDtypeStruct(part.sha...  36.6 us
    dot_general x6, matrix products, dot3(): jnp.dot(left, right, precision=lax.Precision.HIGH, preferred_element_type...  16.2 us
    unnamed x9, local copies, waits for them, and re-layouts  12.9 us
    pad x1, local copies, waits for them, and re-layouts, local(): jnp.pad(jnp.transpose(adjoint, (1, 2, 0)), ((0, 0), (0, 0), (0, WIDE - se...  5.65 us
    dot_general x1, matrix products, local(): lax.dot_general(inverse, smoothed, (((1,), (2,)), ((), ())), preferred_el...  4.3 us
    convert_element_type x1, local copies, waits for them, and re-layouts, local(): return gain_field.astype(jnp.bfloat16)  3.04 us

profile of v2, /device:TPU:1, one launch (start us, length us, event | category | flops | bytes accessed | tf_op | source)
XLA Modules:
  0.0 143.3 jit_solution(12556211814764951174)
XLA Ops:
  0.0 0.7 broadcast_subtract_fusion
  0.7 1.3 fusion.3
  2.0 0.7 multiply_multiply_fusion
  2.7 0.6 reshape.7.variance
  3.3 8.9 %copy.6 = bf16[600,32,128]{0,2,1:T(8,128)(2,1)} copy(bf16[600,32,128]{2,1,0:T(8,128)(2,1)} %param.5) | data formatting | bytes 9830400 | tf_op args[0]
  12.2 5.7 %pad.12.field = bf16[32,128,640]{2,1,0:T(8,128)(2,1)} pad(bf16[32,128,600]{2,1,0:T(8,128)(2,1)} %bitcast.15, bf16[]{:T(256)} %constant.6.clone.1), padding=0_0x0_0x0_40 | pad | bytes 10158082 | tf_op jit(solution)/shard_map/jit(_pad)/pad | solution.py:446
  17.8 59.5 %smooth_and_gram.1 = (bf16[32,128,640]{2,1,0:T(8,128)(2,1)}, f32[3072,128]{1,0:T(8,128)}) custom-call(bf16[32,128,640]{2,1,0:T(8,128)(2,1)} %pad.12.field, f32[32,128]{1,0:T(8,128)} %depth.1, f32[1,640]{1,0:T(1,128)} %reshape.7.variance), custom_call_target="tpu_custom_call" | custom-call | tf_op jit(solution)/shard_map/smooth_and_gram/pallas_call | solution.py:401
  77.3 36.6 %gram_all_reduce.1 = f32[3072,128]{1,0:T(8,128)} custom-call(f32[3072,128]{1,0:T(8,128)} %get-tuple-element.7.part), custom_call_target="tpu_custom_call" | custom-call | tf_op jit(solution)/shard_map/gram_all_reduce/pallas_call | solution.py:143
  113.9 1.0 slice_dynamic-update-slice_fusion.4
  114.9 1.0 slice_dynamic-update-slice_fusion.3
  115.9 1.0 slice_dynamic-update-slice_fusion.2
  116.9 1.0 slice_dynamic-update-slice_fusion.1
  117.9 1.0 slice_dynamic-update-slice_fusion
  118.9 0.2 abs_reduce_fusion
  119.1 0.6 reduce_max.9
  119.7 3.1 %fusion.7 = f32[600,600]{1,0:T(8,128)S(1)} fusion(f32[600,640]{1,0:T(8,128)S(1)} %slice_dynamic-update-slice_fusion, f32[]{:T(128)} %reduce_max.9), kind=kOutput, calls=%fused_computation.15 | convolution fusion | flops 1297440000 | bytes 2976004 | tf_op jit(solution)/shard_map/dot_general | solution.py:165
  122.8 3.1 %convolution_add_fusion.2 = f32[600,600]{1,0:T(8,128)S(1)} fusion(f32[600,600]{1,0:T(8,128)S(1)} %fusion.7, f32[]{:T(128)} %reduce_max.9, f32[600,640]{1,0:T(8,128)S(1)} %slice_dynamic-update-slice_fusion), kind=kOutput, calls=%fused_computation.5 | convolution fusion | flops 1298520064 | bytes 4416004 | tf_op jit(solution)/shard_map/dot_general | solution.py:165
  125.9 2.4 %fusion.10 = f32[600,600]{1,0:T(8,128)S(1)} fusion(f32[600,600]{1,0:T(8,128)S(1)} %fusion.7), kind=kOutput, calls=%fused_computation.28 | convolution fusion | flops 1296000000 | bytes 2880000 | tf_op jit(solution)/shard_map/dot_general | solution.py:165
  128.3 0.0 slice-start
  128.3 2.5 %convolution_add_fusion.1 = f32[600,600]{1,0:T(8,128)S(1)} fusion(f32[600,600]{1,0:T(8,128)S(1)} %convolution_add_fusion.2, f32[600,600]{1,0:T(8,128)S(1)} %fusion.10), kind=kOutput, calls=%fused_computation.4 | convolution fusion | flops 1296359936 | bytes 4320000 | tf_op jit(solution)/shard_map/dot_general | solution.py:165
  130.8 0.0 slice-start.1
  130.8 2.6 %fusion.11 = f32[600,600]{1,0:T(8,128)S(1)} fusion(f32[600,600]{1,0:T(8,128)S(1)} %fusion.10), kind=kOutput, calls=%fused_computation.29 | convolution fusion | flops 1296000000 | bytes 2880000 | tf_op jit(solution)/shard_map/dot_general | solution.py:165
  133.5 2.5 %fusion.2 = bf16[600,600]{1,0:T(8,128)(2,1)S(1)} fusion(f32[600,600]{1,0:T(8,128)S(1)} %convolution_add_fusion.1, f32[600,600]{1,0:T(8,128)S(1)} %fusion.11), kind=kOutput, calls=%fused_computation.9 | convolution fusion | flops 1296720000 | bytes 3600000 | tf_op jit(solution)/shard_map/dot_general | solution.py:165
  135.9 0.0 slice-done
  135.9 0.0 slice-done.1
  136.0 4.3 %convolution_convert_fusion = bf16[600,32,128]{2,0,1:T(8,128)(2,1)S(1)} fusion(bf16[32,128,640]{2,1,0:T(8,128)(2,1)S(1)} %bitcast.17, bf16[600,600]{1,0:T(8,128)(2,1)S(1)} %fusion.2), kind=kOutput, calls=%fused_computation | convolution fusion | flops 3148185600 | bytes 10878080 | tf_op jit(solution)/shard_map/dot_general | solution.py:460
  140.3 3.0 %copy.7 = bf16[600,32,128]{2,1,0:T(8,128)(2,1)} copy(bf16[600,32,128]{2,0,1:T(8,128)(2,1)S(1)} %convolution_convert_fusion) | data formatting | bytes 9830400 | tf_op jit(solution)/shard_map/convert_element_type | solution.py:463
  (2 shorter events, 0.0 us)
Async XLA Ops:
  128.3 7.6 %slice-start = ((s8[5242880]{0:T(1024)(128)(4,1)}), s8[4194304]{0:T(1024)(128)(4,1)S(1)}, s32[]{:S(2)}) async-start(s8[5242880]{0:T(1024)(128)(4,1)} %bitcast.16), calls=%async_computation | async-start | bytes 8388608
  130.8 5.1 %slice-start.1 = ((s8[5242880]{0:T(1024)(128)(4,1)}), s8[1048576]{0:T(1024)(128)(4,1)S(1)}, s32[]{:S(2)}) async-start(s8[5242880]{0:T(1024)(128)(4,1)} %bitcast.16), calls=%async_computation.1 | async-start | bytes 2097152

commit v3 on v2

v3 whole, which is shorter than its diff:
```python
import jax
import jax.numpy as jnp
from jax import lax
from jax.experimental import pallas as pl
from jax.experimental.pallas import tpu as pltpu
from jax.sharding import PartitionSpec as P

SWEEPS = 4
MESH = pl.DeviceIdType.MESH
LANES = 128
CLASSES = 3
CLASS_ROWS = 768


diffusion_step = 0.06


def position():
    gx, gy = lax.axis_index("gx"), lax.axis_index("gy")
    x, y, z, core = gy // 4, ((gy // 2) % 2) * 2 + gx // 4, gx % 4, gy % 2
    return [x, y, z], core


def device(place, core):
    x, y, z = place
    return ((y % 2) * 4 + z, x * 4 + (y // 2) * 2 + core)


def moved(place, axis, step):
    there = list(place)
    there[axis] = (place[axis] + step) % 4
    return there


def all_reduce_kernel(part, total, half_in, q_in, e_in, p_in, half, quarter, send, recv):
    place, core = position()
    barrier = pltpu.get_barrier_semaphore()
    pl.semaphore_signal(barrier, inc=1, device_id=device(place, 1 - core), device_id_type=MESH)
    for axis in range(3):
        for step in (1, 2, 3):
            pl.semaphore_signal(
                barrier, inc=1, device_id=device(moved(place, axis, step), core), device_id_type=MESH
            )
    pl.semaphore_wait(barrier, 10)

    def rows(start, size):
        return pl.ds(pl.multiple_of(start, 8), size)

    def push(src, dst, sem, place_to, core_to):
        copy = pltpu.make_async_remote_copy(
            src_ref=src,
            dst_ref=dst,
            send_sem=send.at[sem],
            recv_sem=recv.at[sem],
            device_id=device(place_to, core_to),
            device_id_type=MESH,
        )
        copy.start()
        return copy

    sizes = (CLASS_ROWS // 2, CLASS_ROWS // 8, CLASS_ROWS // 32)
    started = []
    pending = {}
    for q in range(CLASSES):
        copy = push(
            part.at[rows(q * CLASS_ROWS + (1 - core) * sizes[0], sizes[0])],
            half_in.at[q],
            q,
            place,
            1 - core,
        )
        pending[q, 0] = [copy]
    slots = (None, q_in, e_in)
    sums = (half, quarter)
    base = {q: q * CLASS_ROWS + core * sizes[0] for q in range(CLASSES)}
    for stage in range(3):
        for q in range(CLASSES):
            for copy in pending[q, stage]:
                copy.wait_recv()
            started += pending[q, stage]
            size = sizes[stage]
            if stage == 0:
                value = part[rows(base[q], size), :] + half_in[q]
            else:
                axis = (q + stage - 1) % 3
                value = sums[stage - 1][q, rows(place[axis] * size, size), :]
                for slot in range(3):
                    value = value + slots[stage][q, slot]
                base[q] = base[q] + place[axis] * size
            axis = (q + stage) % 3
            if stage < 2:
                sums[stage][q] = value
                size = sizes[stage + 1]
                pending[q, stage + 1] = [
                    push(
                        sums[stage].at[q, rows(((place[axis] + step) % 4) * size, size)],
                        slots[stage + 1].at[q, step - 1],
                        3 + (stage * CLASSES + q) * 3 + step - 1,
                        moved(place, axis, step),
                        core,
                    )
                    for step in (1, 2, 3)
                ]
            else:
                mine = p_in.at[q, place[axis]]
                p_in[q, place[axis]] = value
                pending[q, 3] = [
                    push(
                        mine,
                        mine,
                        3 + (stage * CLASSES + q) * 3 + step - 1,
                        moved(place, axis, step),
                        core,
                    )
                    for step in (1, 2, 3)
                ]
    for q in range(CLASSES):
        for copy in pending[q, 3]:
            copy.wait_recv()
        started += pending[q, 3]
        value = (p_in[q, 0] + p_in[q, 1]) + (p_in[q, 2] + p_in[q, 3])
        total[rows(base[q], sizes[2]), :] = value
    sem0 = 3 + 27
    for stage in (2, 1, 0):
        for q in range(CLASSES):
            if stage < 2:
                for copy in pending[q, "g", stage + 1]:
                    copy.wait_recv()
                started += pending[q, "g", stage + 1]
                axis = (q + stage) % 3
                base[q] = base[q] - place[axis] * sizes[stage + 1]
            size = sizes[stage]
            here = total.at[rows(base[q], size)]
            if stage == 0:
                pending[q, "g", 0] = [push(here, here, sem0 + 27 + q, place, 1 - core)]
                continue
            axis = (q + stage - 1) % 3
            pending[q, "g", stage] = [
                push(
                    here,
                    here,
                    sem0 + ((stage - 1) * CLASSES + q) * 3 + step - 1,
                    moved(place, axis, step),
                    core,
                )
                for step in (1, 2, 3)
            ]
    for q in range(CLASSES):
        for copy in pending[q, "g", 0]:
            copy.wait_recv()
        started += pending[q, "g", 0]
    for copy in started:
        copy.wait_send()


def all_reduced(part):
    vmem = pl.BlockSpec(memory_space=pltpu.VMEM)
    f32 = jnp.float32
    return pl.pallas_call(
        all_reduce_kernel,
        out_shape=jax.ShapeDtypeStruct(part.shape, f32),
        in_specs=[vmem],
        out_specs=vmem,
        scratch_shapes=[
            pltpu.VMEM((CLASSES, CLASS_ROWS // 2, LANES), f32),
            pltpu.VMEM((CLASSES, 3, CLASS_ROWS // 8, LANES), f32),
            pltpu.VMEM((CLASSES, 3, CLASS_ROWS // 32, LANES), f32),
            pltpu.VMEM((CLASSES, 4, CLASS_ROWS // 32, LANES), f32),
            pltpu.VMEM((CLASSES, CLASS_ROWS // 2, LANES), f32),
            pltpu.VMEM((CLASSES, CLASS_ROWS // 8, LANES), f32),
            pltpu.SemaphoreType.DMA((60,)),
            pltpu.SemaphoreType.DMA((60,)),
        ],
        compiler_params=pltpu.CompilerParams(collective_id=0, has_side_effects=True),
        name="gram_all_reduce",
    )(part)


SENSORS = 600
WIDE = 640
CHUNKS = WIDE // LANES
BLOCKS = [(i, j) for i in range(CHUNKS) for j in range(i, CHUNKS)]
TOP = 16
BLOCK = 48
DIRECTIONS = ((0, 1), (0, -1), (1, 0), (-1, 0), (1, 1), (1, -1), (-1, 1), (-1, -1))


def smooth_kernel(
    adjoint, depth, sensor_row, sensor_column, noise, smoothed_out, gram,
    smoothed, level0, coefficient, levels, total, natural, west, east, low_rows, high_rows,
    low_send, high_send, edge_send, depths, send, recv, load_sem, out_sem,
):
    gx, gy = lax.axis_index("gx"), lax.axis_index("gy")
    sensors, columns, rows = adjoint.shape
    f32, bf16 = jnp.float32, jnp.bfloat16
    loads = []
    for chunk in range(CHUNKS):
        count = min(LANES, sensors - chunk * LANES)
        loads.append(
            pltpu.make_async_copy(
                adjoint.at[pl.ds(chunk * LANES, count)],
                natural.at[chunk, pl.ds(0, count)],
                load_sem.at[chunk],
            )
        )
        loads[-1].start()
    spare = CHUNKS * LANES - sensors
    natural[CHUNKS - 1, pl.ds(LANES - spare, spare)] = jnp.zeros((spare, columns, rows), bf16)

    def neighbour(step):
        return (lax.rem(gx + step[0] + 8, 8), lax.rem(gy + step[1] + 16, 16))

    barrier = pltpu.get_barrier_semaphore()
    for step in DIRECTIONS:
        pl.semaphore_signal(barrier, inc=1, device_id=neighbour(step), device_id_type=MESH)

    upper = lax.broadcasted_iota(jnp.int32, (8, LANES), 0) < 4

    def turn(chunk, half):
        part = natural[chunk, :, pl.ds(pl.multiple_of(half * 16, 16), 16), :]
        level0[pl.ds(half * 16 + 4, 16), chunk, pl.ds(TOP, rows), :] = jnp.transpose(
            part.astype(f32), (1, 2, 0)
        )

    def pack(chunk, group):
        first, last = [], []
        for pair in (0, 1):
            at = group * 4 + pair * 2 + 4
            a, b = [level0[at + odd, chunk, pl.ds(TOP, 8), :] for odd in (0, 1)]
            first.append(jnp.where(upper, a, pltpu.roll(b, 4, 0)))
            a, b = [level0[at + odd, chunk, pl.ds(TOP + rows - 8, 8), :] for odd in (0, 1)]
            last.append(jnp.where(upper, pltpu.roll(a, 4, 0), b))
        at = pl.ds(pl.multiple_of(group * 16, 16), 16)
        low_send[chunk, at, :] = jnp.concatenate(first).astype(bf16)
        high_send[chunk, at, :] = jnp.concatenate(last).astype(bf16)

    def push(src, dst, sem, step):
        copy = pltpu.make_async_remote_copy(
            src_ref=src,
            dst_ref=dst,
            send_sem=send.at[sem],
            recv_sem=recv.at[sem],
            device_id=neighbour(step),
            device_id_type=MESH,
        )
        copy.start()
        return copy

    n4 = columns * 4
    row_copies = []
    depth_copies = []
    for chunk in range(CHUNKS):
        loads[chunk].wait()
        lax.fori_loop(0, columns // 16, lambda half, _: (turn(chunk, half), 0)[1], 0)
        lax.fori_loop(0, columns // 4, lambda group, _: (pack(chunk, group), 0)[1], 0)
        if chunk == 0:
            pl.semaphore_wait(barrier, 8)
            depth_copies = [push(depth, depths.at[k], k, DIRECTIONS[k]) for k in range(8)]
        inner = pl.ds(16, n4)
        row_copies += [
            push(high_send.at[chunk], low_rows.at[chunk, inner], 14 + chunk, (1, 0)),
            push(low_send.at[chunk], high_rows.at[chunk, inner], 19 + chunk, (-1, 0)),
        ]

    def edges(column, _):
        edge_send[column] = level0[column + 4, :, pl.ds(TOP, rows), :].astype(bf16)
        edge_send[column + 4] = level0[column + columns, :, pl.ds(TOP, rows), :].astype(bf16)
        return 0

    lax.fori_loop(0, 4, edges, 0)
    front, back = pl.ds(0, 16), pl.ds(n4 + 16, 16)
    final = pl.ds(n4 - 16, 16)
    halo_copies = [
        push(edge_send.at[pl.ds(4, 4)], west, 8, (0, 1)),
        push(edge_send.at[pl.ds(0, 4)], east, 9, (0, -1)),
        push(high_send.at[:, final], low_rows.at[:, front], 10, (1, 1)),
        push(high_send.at[:, front], low_rows.at[:, back], 11, (1, -1)),
        push(low_send.at[:, final], high_rows.at[:, front], 12, (-1, 1)),
        push(low_send.at[:, front], high_rows.at[:, back], 13, (-1, -1)),
    ]

    site_column = sensor_column[...].reshape(1, sensors) - gy * columns
    site_row = sensor_row[...].reshape(1, sensors) - gx * rows
    sigma = noise[...].reshape(1, sensors)
    pick = lax.broadcasted_iota(jnp.int32, (columns, sensors), 0) == site_column
    along = lax.dot_general(
        depth[...],
        pick.astype(f32),
        (((0,), (0,)), ((), ())),
        precision=lax.Precision.HIGHEST,
        preferred_element_type=f32,
    )
    pick = lax.broadcasted_iota(jnp.int32, (rows, sensors), 0) == site_row
    variance = sigma * sigma * jnp.sum(jnp.where(pick, along, 0.0), axis=0, keepdims=True)
    variance = jnp.concatenate([variance, jnp.zeros((1, spare), f32)], axis=1)

    for copy in depth_copies:
        copy.wait_recv()
    inside_x = {1: gx > 0, -1: gx < 7, 0: gx >= 0}
    inside_y = {1: gy > 0, -1: gy < 15, 0: gy >= 0}

    def tile(step):
        if step == (0, 0):
            return depth[...]
        keep = jnp.logical_and(inside_x[step[0]], inside_y[step[1]])
        return depths[DIRECTIONS.index(step)] * jnp.where(keep, 1.0, 0.0)

    turned = []
    for dx in (1, 0, -1):
        stack = jnp.concatenate(
            [
                tile((dx, 1))[columns - 8 :],
                tile((dx, 0)),
                tile((dx, -1))[:8],
                jnp.zeros((LANES - columns - 16, rows), f32),
            ]
        )
        turned.append(jnp.transpose(stack))
    here = jnp.concatenate([turned[0][rows - TOP :], turned[1], turned[2][:TOP]])
    height = rows + 2 * TOP
    others = (
        pltpu.roll(here, height - 1, 0),
        pltpu.roll(here, 1, 0),
        pltpu.roll(here, LANES - 1, 1),
        pltpu.roll(here, 1, 1),
    )
    weights = [diffusion_step * (0.5 * (here + other)) for other in others]
    kept = [jnp.where(other > 0.0, w, 0.0) for other, w in zip(others, weights)]
    centre = 1.0 - (weights[0] + weights[1] + weights[2] + weights[3])
    for index, value in enumerate([centre] + kept):
        value = value[8 : height - 8]
        for column in range(columns + 6):
            coefficient[index, column] = jnp.broadcast_to(
                value[:, column + 5 : column + 6], (height - 16, LANES)
            )

    def edge(column, _):
        level0[column, :, pl.ds(TOP, rows), :] = west[column].astype(f32)
        level0[column + columns + 4, :, pl.ds(TOP, rows), :] = east[column].astype(f32)
        return 0

    def rims(group, _):
        at = pl.ds(pl.multiple_of(group * 16, 16), 16)
        for chunk in range(CHUNKS):
            low, high = low_rows[chunk, at, :].astype(f32), high_rows[chunk, at, :].astype(f32)
            for pair in (0, 1):
                a, b = low[pair * 8 : pair * 8 + 8], high[pair * 8 : pair * 8 + 8]
                column = group * 4 + pair * 2
                before, after = pl.ds(TOP - 8, 8), pl.ds(TOP + rows, 8)
                level0[column, chunk, before, :] = pltpu.roll(a, 4, 0)
                level0[column + 1, chunk, before, :] = a
                level0[column, chunk, after, :] = b
                level0[column + 1, chunk, after, :] = pltpu.roll(b, 4, 0)
        return 0

    for copy in row_copies:
        copy.wait_recv()
    lax.fori_loop(1, columns // 4 + 1, rims, 0)

    def sweep(read, write, column, first, last):
        for start in range(first, last, BLOCK):
            size = min(BLOCK, last - start)
            k = [coefficient[index, column, pl.ds(8 + start, size), :] for index in range(5)]
            for chunk in range(CHUNKS):
                at = TOP + start
                write(
                    chunk,
                    start,
                    size,
                    k[0] * read(1, chunk, at, size)
                    + k[1] * read(1, chunk, at + 1, size)
                    + k[2] * read(1, chunk, at - 1, size)
                    + k[3] * read(2, chunk, at, size)
                    + k[4] * read(0, chunk, at, size),
                )

    up = columns + 2

    def wave(t, _):
        @pl.when(t == up - 4)
        def _():
            for copy in halo_copies:
                copy.wait_recv()
            lax.fori_loop(0, 4, edge, 0)
            rims(0, 0)
            rims(columns // 4 + 1, 0)

        down = (t >= up).astype(jnp.int32)
        sign = 1 - 2 * down
        first = jnp.where(t >= up, up - t, t + 1)
        order = jnp.where(t >= up, t - up + 2, t + 1)
        near, middle, far = [lax.rem(order + k, 3) for k in (0, 2, 1)]
        slots = (jnp.where(t >= up, near, far), middle, jnp.where(t >= up, far, near))

        def read_first(which, chunk, at, size):
            return level0[first + 3 + which, chunk, pl.ds(at, size), :]

        def read_level(level):
            return lambda which, chunk, at, size: levels[
                down, level, slots[which], chunk, pl.ds(at, size), :
            ]

        def write_level(level):
            def write(chunk, start, size, value):
                levels[down, level, near, chunk, pl.ds(TOP + start, size), :] = value

            return write

        sweep(read_first, write_level(0), first + 3, -8, rows + 8)
        sweep(read_level(0), write_level(1), first + 3 - sign, -8, rows + 8)
        sweep(read_level(1), write_level(2), first + 3 - 2 * sign, -8, rows + 8)

        @pl.when(t < 6)
        def _():
            level = lax.div(t, 2)
            levels[1, level, lax.rem(t + 1, 2)] = levels[0, level, near]

        @pl.when(t >= 6)
        def _():
            def write(chunk, start, size, value):
                smoothed[
                    first - 3 * sign, pl.ds(start, size), pl.ds(chunk * LANES, LANES)
                ] = value.astype(bf16)

            sweep(read_level(2), write, first + 3 - 3 * sign, 0, rows)

        return 0

    lax.fori_loop(0, up + 4, wave, 0)
    out_copy = pltpu.make_async_copy(smoothed, smoothed_out, out_sem)
    out_copy.start()

    total[...] = jnp.zeros_like(total)

    def accumulate(group, _):
        part = smoothed[pl.ds(group * 8, 8)].reshape(8 * rows, WIDE)
        for chunk in range(CHUNKS):
            at = chunk * LANES
            total[pl.ds(at, LANES), pl.ds(at, WIDE - at)] += lax.dot_general(
                part[:, at : at + LANES],
                part[:, at:],
                (((0,), (0,)), ((), ())),
                preferred_element_type=f32,
            )
        return 0

    lax.fori_loop(0, columns // 8, accumulate, 0)
    inverse_cells = 1.0 / (columns * rows * 128)
    diagonal = lax.broadcasted_iota(jnp.int32, (LANES, LANES), 0) == lax.broadcasted_iota(
        jnp.int32, (LANES, LANES), 1
    )
    for at, (i, j) in enumerate(BLOCKS):
        value = total[pl.ds(i * LANES, LANES), pl.ds(j * LANES, LANES)] * inverse_cells
        if i == j:
            part = slice(i * LANES, (i + 1) * LANES)
            value = value + jnp.where(diagonal, variance[:, part], 0.0)
        gram[pl.ds(at * LANES, LANES), :] = value
    unused = gram.shape[0] - len(BLOCKS) * LANES
    gram[pl.ds(len(BLOCKS) * LANES, unused), :] = jnp.zeros((unused, LANES), f32)
    out_copy.wait()
    for copy in depth_copies + row_copies + halo_copies:
        copy.wait_send()


def smoothed_and_gram(adjoint, depth, sensor_row, sensor_column, noise):
    vmem = pl.BlockSpec(memory_space=pltpu.VMEM)
    whole = pl.BlockSpec(memory_space=pl.ANY)
    f32, bf16 = jnp.float32, jnp.bfloat16
    _, columns, rows = adjoint.shape
    height = rows + 2 * TOP
    rim = pltpu.VMEM((CHUNKS, (columns + 8) * 4, LANES), bf16)
    return pl.pallas_call(
        smooth_kernel,
        out_shape=(
            jax.ShapeDtypeStruct((columns, rows, WIDE), bf16),
            jax.ShapeDtypeStruct((CLASSES * CLASS_ROWS, LANES), f32),
        ),
        in_specs=[whole] + [vmem] * 4,
        out_specs=(whole, vmem),
        scratch_shapes=[
            pltpu.VMEM((columns, rows, WIDE), bf16),
            pltpu.VMEM((columns + 8, CHUNKS, height, LANES), f32),
            pltpu.VMEM((5, columns + 6, height - 16, LANES), f32),
            pltpu.VMEM((2, 3, 3, CHUNKS, height, LANES), f32),
            pltpu.VMEM((WIDE, WIDE), f32),
            pltpu.VMEM((CHUNKS, LANES, columns, rows), bf16),
            pltpu.VMEM((4, CHUNKS, rows, LANES), bf16),
            pltpu.VMEM((4, CHUNKS, rows, LANES), bf16),
            rim,
            rim,
            pltpu.VMEM((CHUNKS, columns * 4, LANES), bf16),
            pltpu.VMEM((CHUNKS, columns * 4, LANES), bf16),
            pltpu.VMEM((8, CHUNKS, rows, LANES), bf16),
            pltpu.VMEM((8, columns, rows), f32),
            pltpu.SemaphoreType.DMA((24,)),
            pltpu.SemaphoreType.DMA((24,)),
            pltpu.SemaphoreType.DMA((CHUNKS,)),
            pltpu.SemaphoreType.DMA,
        ],
        compiler_params=pltpu.CompilerParams(
            collective_id=1, has_side_effects=True, vmem_limit_bytes=66_000_000
        ),
        name="smooth_and_gram",
    )(adjoint, depth, sensor_row, sensor_column, noise)


GROUP = 16


def split(value):
    high = value.astype(jnp.bfloat16)
    return high, (value - high.astype(jnp.float32)).astype(jnp.bfloat16)


def gain_kernel(stacked, smoothed_in, out, left, right, plane, smoothed, spread, ready, sems):
    f32, bf16 = jnp.float32, jnp.bfloat16
    columns, rows, _ = smoothed.shape
    load = pltpu.make_async_copy(smoothed_in, smoothed, sems.at[2])
    load.start()
    whole = plane.at[1]
    for at, (i, j) in enumerate(BLOCKS):
        block = stacked[pl.ds(at * LANES, LANES), :]
        size = min(LANES, SENSORS - i * LANES)
        whole[pl.ds(i * LANES, size), pl.ds(j * LANES, LANES)] = block[:size]
        if i != j:
            size = min(LANES, SENSORS - j * LANES)
            whole[pl.ds(j * LANES, size), pl.ds(i * LANES, LANES)] = jnp.transpose(block)[:size]
    blocks = [whole[:, chunk * LANES : (chunk + 1) * LANES] for chunk in range(CHUNKS)]
    reach = sum(jnp.sum(jnp.abs(block), axis=1, keepdims=True) for block in blocks)
    scale = 1.0 / jnp.max(reach)
    row = lax.broadcasted_iota(jnp.int32, (SENSORS, LANES), 0)
    lane = lax.broadcasted_iota(jnp.int32, (SENSORS, LANES), 1)
    zeros = jnp.zeros((WIDE - SENSORS, WIDE), bf16)

    def store(at, high, low):
        right[pl.ds(0, SENSORS), at] = high
        right[pl.ds(WIDE, SENSORS), at] = high
        right[pl.ds(2 * WIDE, SENSORS), at] = low

    for k in range(3):
        for half in range(2):
            right[pl.ds(k * WIDE + SENSORS, WIDE - SENSORS), pl.ds(half * WIDE, WIDE)] = zeros
    inverse = plane.at[1]
    for chunk, block in enumerate(blocks):
        diagonal = jnp.where(row == lane + chunk * LANES, 1.0, 0.0)
        residual = diagonal - block * scale
        at = pl.ds(chunk * LANES, LANES)
        plane[0, :, at] = residual
        inverse[:, at] = (diagonal + residual) * scale

    def product(width):
        value = plane[0]
        high, low = split(value)
        left[:, pl.ds(0, WIDE)] = high
        left[:, pl.ds(WIDE, WIDE)] = low
        left[:, pl.ds(2 * WIDE, WIDE)] = high
        store(pl.ds(0, WIDE), high, low)
        if width > WIDE:
            high, low = split(inverse[...])
            store(pl.ds(WIDE, WIDE), high, low)
        return jnp.dot(left[...], right[:, pl.ds(0, width)], preferred_element_type=f32)

    plane[0] = product(WIDE)
    for _ in range(2):
        both = product(2 * WIDE)
        plane[0] = both[:, :WIDE]
        inverse[...] = inverse[...] + both[:, WIDE:]
    high, low = split(plane[0])
    left[:, pl.ds(0, WIDE)] = high
    left[:, pl.ds(WIDE, WIDE)] = low
    left[:, pl.ds(2 * WIDE, WIDE)] = high
    high, low = split(inverse[...])
    store(pl.ds(0, WIDE), high, low)
    final = inverse[...] + jnp.dot(
        left[...], right[:, pl.ds(0, WIDE)], preferred_element_type=f32
    )
    left[:, pl.ds(0, WIDE)] = final.astype(bf16)

    load.wait()
    stores = []
    for group in range(columns // GROUP):
        for pair in range(GROUP // 2):
            field = smoothed[pl.ds(group * GROUP + pair * 2, 2)].reshape(2 * rows, WIDE)
            value = lax.dot_general(
                left[:, pl.ds(0, WIDE)],
                field,
                (((1,), (1,)), ((), ())),
                preferred_element_type=f32,
            )
            for odd in (0, 1):
                spread[pl.ds(pair * 2 + odd, SENSORS, stride=GROUP), :] = value[
                    :, odd * rows : (odd + 1) * rows
                ]
        ready[group] = spread[...].reshape(SENSORS, GROUP, rows).astype(bf16)
        stores.append(
            pltpu.make_async_copy(
                ready.at[group], out.at[:, pl.ds(group * GROUP, GROUP), :], sems.at[group]
            )
        )
        stores[-1].start()
    for store in stores:
        store.wait()


def gains(stacked, smoothed):
    vmem = pl.BlockSpec(memory_space=pltpu.VMEM)
    columns, rows, _ = smoothed.shape
    return pl.pallas_call(
        gain_kernel,
        out_shape=jax.ShapeDtypeStruct((SENSORS, columns, rows), jnp.bfloat16),
        in_specs=[vmem, pl.BlockSpec(memory_space=pl.ANY)],
        out_specs=pl.BlockSpec(memory_space=pl.ANY),
        scratch_shapes=[
            pltpu.VMEM((SENSORS, 3 * WIDE), jnp.bfloat16),
            pltpu.VMEM((3 * WIDE, 2 * WIDE), jnp.bfloat16),
            pltpu.VMEM((2, SENSORS, WIDE), jnp.float32),
            pltpu.VMEM(smoothed.shape, jnp.bfloat16),
            pltpu.VMEM((SENSORS * GROUP, LANES), jnp.float32),
            pltpu.VMEM((columns // GROUP, SENSORS, GROUP, rows), jnp.bfloat16),
            pltpu.SemaphoreType.DMA((3,)),
        ],
        compiler_params=pltpu.CompilerParams(vmem_limit_bytes=66_000_000),
        name="inverse_and_gain",
    )(stacked, smoothed)


def local(adjoint, seafloor_depth, sensor_row, sensor_column, noise_sigma):
    smoothed, stacked = smoothed_and_gram(
        adjoint, seafloor_depth, sensor_row, sensor_column, noise_sigma
    )
    return gains(all_reduced(stacked), smoothed)


def solution(mesh):
    in_specs = (P(None, "gy", "gx"), P("gy", "gx"), P(), P(), P())
    out_specs = P(None, "gy", "gx")
    return jax.shard_map(local, mesh=mesh, in_specs=in_specs, out_specs=out_specs, check_vma=False)
```

time: 144 us -> 102 us (0.71)
  local copies, waits for them, and re-layouts: 23.2 us -> 0 us
  matrix products: 21.7 us -> 0 us
  Pallas kernels: 96.1 us -> 102 us
  other arithmetic: 2.21 us -> 0 us
    dot_general x8 -> x0, matrix products: 21.7 us -> none  [the longest x6 16.2 us: dot3(): jnp.dot(left, right, precision=lax.Precision.HIGH, preferred_element_type...]
    unnamed x9 -> x0, local copies, waits for them, and re-layouts: 12.9 us -> none
    pallas_call x1 -> x2, Pallas kernels: 59.5 us -> 65.9 us  [the longest x1 43.6 us: smoothed_and_gram(): pl.pallas_call(smooth_kernel, out_shape=(jax.ShapeDtypeStruct((columns, r...]
    pad x2 -> x0, local copies, waits for them, and re-layouts: 5.66 us -> none  [the longest x1 5.65 us: local(): jnp.pad(jnp.transpose(adjoint, (1, 2, 0)), ((0, 0), (0, 0), (0, WIDE - se...]
    convert_element_type x1 -> x0, local copies, waits for them, and re-layouts: 3.04 us -> none  [local(): return gain_field.astype(jnp.bfloat16)]
where the time goes in v3:
time: 102 us
  Pallas kernels  102 us (100%)
    pallas_call x1, Pallas kernels, smoothed_and_gram(): pl.pallas_call(smooth_kernel, out_shape=(jax.ShapeDtypeStruct((columns, r...  43.6 us
    pallas_call x1, Pallas kernels, all_reduced(): pl.pallas_call(all_reduce_kernel, out_shape=jax.ShapeDtypeStruct(part.sha...  35.9 us
    pallas_call x1, Pallas kernels, gains(): pl.pallas_call(gain_kernel, out_shape=jax.ShapeDtypeStruct((SENSORS, colu...  22.3 us

profile of v3, /device:TPU:1, one launch (start us, length us, event | category | flops | bytes accessed | tf_op | source)
XLA Modules:
  0.0 102.0 jit_solution(17217138733469406685)
XLA Ops:
  0.0 43.6 %smooth_and_gram.1 = (bf16[32,128,640]{2,1,0:T(8,128)(2,1)}, f32[2304,128]{1,0:T(8,128)}) custom-call(bf16[600,32,128]{2,1,0:T(8,128)(2,1)} %adjoint.1, f32[32,128]{1,0:T(8,128)} %depth.1, s32[600]{0:T(1024)} %sensor_row.1, s32[600]{0:T(1024)} %sensor_column.1, f32[600]{0:T(1024)} %noise.1), custom_call_target="tpu_custom_call" | custom-call | tf_op jit(solution)/shard_map/smooth_and_gram/pallas_call | solution.py:472
  43.6 35.9 %gram_all_reduce.1.stacked = f32[2304,128]{1,0:T(8,128)} custom-call(f32[2304,128]{1,0:T(8,128)} %get-tuple-element.7.part), custom_call_target="tpu_custom_call" | custom-call | tf_op jit(solution)/shard_map/gram_all_reduce/pallas_call | solution.py:159
  79.5 22.3 %inverse_and_gain.1 = bf16[600,32,128]{2,1,0:T(8,128)(2,1)} custom-call(f32[2304,128]{1,0:T(8,128)} %gram_all_reduce.1.stacked, bf16[32,128,640]{2,1,0:T(8,128)(2,1)} %get-tuple-element.8.smoothed_in), custom_call_target="tpu_custom_call" | custom-call | tf_op jit(solution)/shard_map/inverse_and_gain/pallas_call | solution.py:608

commit v4 on v3

--- a/solution.py
+++ b/solution.py
@@ -32,21 +32,27 @@
     return there
 
 
-def all_reduce_kernel(part, total, half_in, q_in, e_in, p_in, half, quarter, send, recv):
-    place, core = position()
-    barrier = pltpu.get_barrier_semaphore()
+def greet(barrier, place, core):
     pl.semaphore_signal(barrier, inc=1, device_id=device(place, 1 - core), device_id_type=MESH)
     for axis in range(3):
         for step in (1, 2, 3):
             pl.semaphore_signal(
                 barrier, inc=1, device_id=device(moved(place, axis, step), core), device_id_type=MESH
             )
-    pl.semaphore_wait(barrier, 10)
+
+
+def all_reduce(part, total, half_in, q_in, e_in, p_in, half, quarter, send, recv):
+    place, core = position()
+    size0, size1, size2 = CLASS_ROWS // 2, CLASS_ROWS // 8, CLASS_ROWS // 32
+    classes = range(CLASSES)
 
     def rows(start, size):
         return pl.ds(pl.multiple_of(start, 8), size)
 
-    def push(src, dst, sem, place_to, core_to):
+    started = []
+
+    def push(src, dst, place_to, core_to):
+        sem = len(started)
         copy = pltpu.make_async_remote_copy(
             src_ref=src,
             dst_ref=dst,
@@ -56,124 +62,86 @@
             device_id_type=MESH,
         )
         copy.start()
+        started.append(copy)
         return copy
 
-    sizes = (CLASS_ROWS // 2, CLASS_ROWS // 8, CLASS_ROWS // 32)
-    started = []
-    pending = {}
-    for q in range(CLASSES):
-        copy = push(
-            part.at[rows(q * CLASS_ROWS + (1 - core) * sizes[0], sizes[0])],
-            half_in.at[q],
-            q,
-            place,
-            1 - core,
-        )
-        pending[q, 0] = [copy]
-    slots = (None, q_in, e_in)
-    sums = (half, quarter)
-    base = {q: q * CLASS_ROWS + core * sizes[0] for q in range(CLASSES)}
-    for stage in range(3):
-        for q in range(CLASSES):
-            for copy in pending[q, stage]:
-                copy.wait_recv()
-            started += pending[q, stage]
-            size = sizes[stage]
-            if stage == 0:
-                value = part[rows(base[q], size), :] + half_in[q]
-            else:
-                axis = (q + stage - 1) % 3
-                value = sums[stage - 1][q, rows(place[axis] * size, size), :]
-                for slot in range(3):
-                    value = value + slots[stage][q, slot]
-                base[q] = base[q] + place[axis] * size
-            axis = (q + stage) % 3
-            if stage < 2:
-                sums[stage][q] = value
-                size = sizes[stage + 1]
-                pending[q, stage + 1] = [
-                    push(
-                        sums[stage].at[q, rows(((place[axis] + step) % 4) * size, size)],
-                        slots[stage + 1].at[q, step - 1],
-                        3 + (stage * CLASSES + q) * 3 + step - 1,
-                        moved(place, axis, step),
-                        core,
-                    )
-                    for step in (1, 2, 3)
-                ]
-            else:
-                mine = p_in.at[q, place[axis]]
-                p_in[q, place[axis]] = value
-                pending[q, 3] = [
-                    push(
-                        mine,
-                        mine,
-                        3 + (stage * CLASSES + q) * 3 + step - 1,
-                        moved(place, axis, step),
-                        core,
-                    )
-                    for step in (1, 2, 3)
-                ]
-    for q in range(CLASSES):
-        for copy in pending[q, 3]:
-            copy.wait_recv()
-        started += pending[q, 3]
-        value = (p_in[q, 0] + p_in[q, 1]) + (p_in[q, 2] + p_in[q, 3])
-        total[rows(base[q], sizes[2]), :] = value
-    sem0 = 3 + 27
-    for stage in (2, 1, 0):
-        for q in range(CLASSES):
-            if stage < 2:
-                for copy in pending[q, "g", stage + 1]:
-                    copy.wait_recv()
-                started += pending[q, "g", stage + 1]
-                axis = (q + stage) % 3
-                base[q] = base[q] - place[axis] * sizes[stage + 1]
-            size = sizes[stage]
-            here = total.at[rows(base[q], size)]
-            if stage == 0:
-                pending[q, "g", 0] = [push(here, here, sem0 + 27 + q, place, 1 - core)]
+    def part_of(q, axis, step):
+        return (place[(q + axis) % 3] + step) % 4
+
+    base = [q * CLASS_ROWS + core * size0 for q in classes]
+    other = [q * CLASS_ROWS + (1 - core) * size0 for q in classes]
+    steps = (2, 1, 3)
+    swaps, first, second, third = {}, {}, {}, {}
+    for step in steps + (0,):
+        for q in classes:
+            at = part_of(q, 0, step) * size1
+            swaps[q, step] = push(
+                part.at[rows(other[q] + at, size1)], half_in.at[q, rows(at, size1)], place, 1 - core
+            )
+    mine = {}
+    for step in steps + (0,):
+        for q in classes:
+            swaps[q, step].wait_recv()
+            at = part_of(q, 0, step) * size1
+            value = part[rows(base[q] + at, size1), :] + half_in[q, rows(at, size1), :]
+            if step == 0:
+                mine[q] = value
                 continue
-            axis = (q + stage - 1) % 3
-            pending[q, "g", stage] = [
-                push(
-                    here,
-                    here,
-                    sem0 + ((stage - 1) * CLASSES + q) * 3 + step - 1,
-                    moved(place, axis, step),
-                    core,
-                )
-                for step in (1, 2, 3)
-            ]
-    for q in range(CLASSES):
-        for copy in pending[q, "g", 0]:
-            copy.wait_recv()
-        started += pending[q, "g", 0]
+            half[q, rows(at, size1), :] = value
+            first[q, step] = push(
+                half.at[q, rows(at, size1)],
+                q_in.at[q, step - 1],
+                moved(place, q % 3, step),
+                core,
+            )
+    for q in classes:
+        for step in (1, 3, 2):
+            first[q, step].wait_recv()
+        quarter[q] = (mine[q] + q_in[q, 0]) + (q_in[q, 1] + q_in[q, 2])
+        base[q] = base[q] + part_of(q, 0, 0) * size1
+        for step in steps:
+            second[q, step] = push(
+                quarter.at[q, rows(part_of(q, 1, step) * size2, size2)],
+                e_in.at[q, step - 1],
+                moved(place, (q + 1) % 3, step),
+                core,
+            )
+    for q in classes:
+        for step in (1, 3, 2):
+            second[q, step].wait_recv()
+        here = part_of(q, 2, 0)
+        own = quarter[q, rows(part_of(q, 1, 0) * size2, size2), :]
+        p_in[q, here] = (own + e_in[q, 0]) + (e_in[q, 1] + e_in[q, 2])
+        for step in steps:
+            third[q, step] = push(
+                p_in.at[q, here], p_in.at[q, here], moved(place, (q + 2) % 3, step), core
+            )
+    for q in classes:
+        for step in (1, 3, 2):
+            third[q, step].wait_recv()
+        at = rows(base[q] + part_of(q, 1, 0) * size2, size2)
+        total[at, :] = (p_in[q, 0] + p_in[q, 1]) + (p_in[q, 2] + p_in[q, 3])
+        for step in steps:
+            second[q, step] = push(
+                total.at[at], total.at[at], moved(place, (q + 1) % 3, step), core
+            )
+    last = []
+    for q in classes:
+        for step in (1, 3, 2):
+            second[q, step].wait_recv()
+        at = rows(base[q], size1)
+        for step in steps:
+            first[q, step] = push(total.at[at], total.at[at], moved(place, q % 3, step), core)
+        last.append(push(total.at[at], total.at[at], place, 1 - core))
+    for step in (1, 3, 2):
+        for q in classes:
+            first[q, step].wait_recv()
+            at = rows(q * CLASS_ROWS + core * size0 + part_of(q, 0, -step) * size1, size1)
+            last.append(push(total.at[at], total.at[at], place, 1 - core))
+    for copy in last:
+        copy.wait_recv()
     for copy in started:
         copy.wait_send()
-
-
-def all_reduced(part):
-    vmem = pl.BlockSpec(memory_space=pltpu.VMEM)
-    f32 = jnp.float32
-    return pl.pallas_call(
-        all_reduce_kernel,
-        out_shape=jax.ShapeDtypeStruct(part.shape, f32),
-        in_specs=[vmem],
-        out_specs=vmem,
-        scratch_shapes=[
-            pltpu.VMEM((CLASSES, CLASS_ROWS // 2, LANES), f32),
-            pltpu.VMEM((CLASSES, 3, CLASS_ROWS // 8, LANES), f32),
-            pltpu.VMEM((CLASSES, 3, CLASS_ROWS // 32, LANES), f32),
-            pltpu.VMEM((CLASSES, 4, CLASS_ROWS // 32, LANES), f32),
-            pltpu.VMEM((CLASSES, CLASS_ROWS // 2, LANES), f32),
-            pltpu.VMEM((CLASSES, CLASS_ROWS // 8, LANES), f32),
-            pltpu.SemaphoreType.DMA((60,)),
-            pltpu.SemaphoreType.DMA((60,)),
-        ],
-        compiler_params=pltpu.CompilerParams(collective_id=0, has_side_effects=True),
-        name="gram_all_reduce",
-    )(part)
 
 
 SENSORS = 600
@@ -186,9 +154,9 @@
 
 
 def smooth_kernel(
-    adjoint, depth, sensor_row, sensor_column, noise, smoothed_out, gram,
-    smoothed, level0, coefficient, levels, total, natural, west, east, low_rows, high_rows,
-    low_send, high_send, edge_send, depths, send, recv, load_sem, out_sem,
+    adjoint, depth, sensor_row, sensor_column, noise, smoothed_out, operator,
+    gram, smoothed, level0, coefficient, levels, total, natural, west, east, low_rows, high_rows,
+    low_send, high_send, edge_send, depths, send, recv, load_sem, out_sem, *sums
 ):
     gx, gy = lax.axis_index("gx"), lax.axis_index("gy")
     sensors, columns, rows = adjoint.shape
@@ -213,6 +181,7 @@
     barrier = pltpu.get_barrier_semaphore()
     for step in DIRECTIONS:
         pl.semaphore_signal(barrier, inc=1, device_id=neighbour(step), device_id_type=MESH)
+    greet(barrier, *position())
 
     upper = lax.broadcasted_iota(jnp.int32, (8, LANES), 0) < 4
 
@@ -254,7 +223,7 @@
         lax.fori_loop(0, columns // 16, lambda half, _: (turn(chunk, half), 0)[1], 0)
         lax.fori_loop(0, columns // 4, lambda group, _: (pack(chunk, group), 0)[1], 0)
         if chunk == 0:
-            pl.semaphore_wait(barrier, 8)
+            pl.semaphore_wait(barrier, 18)
             depth_copies = [push(depth, depths.at[k], k, DIRECTIONS[k]) for k in range(8)]
         inner = pl.ds(16, n4)
         row_copies += [
@@ -407,8 +376,14 @@
             return write
 
         sweep(read_first, write_level(0), first + 3, -8, rows + 8)
-        sweep(read_level(0), write_level(1), first + 3 - sign, -8, rows + 8)
-        sweep(read_level(1), write_level(2), first + 3 - 2 * sign, -8, rows + 8)
+
+        @pl.when(t >= 2)
+        def _():
+            sweep(read_level(0), write_level(1), first + 3 - sign, -8, rows + 8)
+
+        @pl.when(t >= 4)
+        def _():
+            sweep(read_level(1), write_level(2), first + 3 - 2 * sign, -8, rows + 8)
 
         @pl.when(t < 6)
         def _():
@@ -457,12 +432,13 @@
         gram[pl.ds(at * LANES, LANES), :] = value
     unused = gram.shape[0] - len(BLOCKS) * LANES
     gram[pl.ds(len(BLOCKS) * LANES, unused), :] = jnp.zeros((unused, LANES), f32)
+    all_reduce(gram, operator, *sums)
     out_copy.wait()
     for copy in depth_copies + row_copies + halo_copies:
         copy.wait_send()
 
 
-def smoothed_and_gram(adjoint, depth, sensor_row, sensor_column, noise):
+def smoothed_and_operator(adjoint, depth, sensor_row, sensor_column, noise):
     vmem = pl.BlockSpec(memory_space=pltpu.VMEM)
     whole = pl.BlockSpec(memory_space=pl.ANY)
     f32, bf16 = jnp.float32, jnp.bfloat16
@@ -478,6 +454,7 @@
         in_specs=[whole] + [vmem] * 4,
         out_specs=(whole, vmem),
         scratch_shapes=[
+            pltpu.VMEM((CLASSES * CLASS_ROWS, LANES), f32),
             pltpu.VMEM((columns, rows, WIDE), bf16),
             pltpu.VMEM((columns + 8, CHUNKS, height, LANES), f32),
             pltpu.VMEM((5, columns + 6, height - 16, LANES), f32),
@@ -496,15 +473,24 @@
             pltpu.SemaphoreType.DMA((24,)),
             pltpu.SemaphoreType.DMA((CHUNKS,)),
             pltpu.SemaphoreType.DMA,
+            pltpu.VMEM((CLASSES, CLASS_ROWS // 2, LANES), f32),
+            pltpu.VMEM((CLASSES, 3, CLASS_ROWS // 8, LANES), f32),
+            pltpu.VMEM((CLASSES, 3, CLASS_ROWS // 32, LANES), f32),
+            pltpu.VMEM((CLASSES, 4, CLASS_ROWS // 32, LANES), f32),
+            pltpu.VMEM((CLASSES, CLASS_ROWS // 2, LANES), f32),
+            pltpu.VMEM((CLASSES, CLASS_ROWS // 8, LANES), f32),
+            pltpu.SemaphoreType.DMA((69,)),
+            pltpu.SemaphoreType.DMA((69,)),
         ],
         compiler_params=pltpu.CompilerParams(
             collective_id=1, has_side_effects=True, vmem_limit_bytes=66_000_000
         ),
-        name="smooth_and_gram",
+        name="smooth_and_reduce",
     )(adjoint, depth, sensor_row, sensor_column, noise)
 
 
 GROUP = 16
+PIECES = 4
 
 
 def split(value):
@@ -515,7 +501,7 @@
 def gain_kernel(stacked, smoothed_in, out, left, right, plane, smoothed, spread, ready, sems):
     f32, bf16 = jnp.float32, jnp.bfloat16
     columns, rows, _ = smoothed.shape
-    load = pltpu.make_async_copy(smoothed_in, smoothed, sems.at[2])
+    load = pltpu.make_async_copy(smoothed_in, smoothed, sems.at[0])
     load.start()
     whole = plane.at[1]
     for at, (i, j) in enumerate(BLOCKS):
@@ -591,13 +577,22 @@
                 spread[pl.ds(pair * 2 + odd, SENSORS, stride=GROUP), :] = value[
                     :, odd * rows : (odd + 1) * rows
                 ]
-        ready[group] = spread[...].reshape(SENSORS, GROUP, rows).astype(bf16)
-        stores.append(
-            pltpu.make_async_copy(
-                ready.at[group], out.at[:, pl.ds(group * GROUP, GROUP), :], sems.at[group]
-            )
-        )
-        stores[-1].start()
+        for piece in range(PIECES):
+            size = SENSORS // PIECES
+            some = pl.ds(piece * size, size)
+            ready[group, some] = (
+                spread[pl.ds(piece * size * GROUP, size * GROUP), :]
+                .reshape(size, GROUP, rows)
+                .astype(bf16)
+            )
+            stores.append(
+                pltpu.make_async_copy(
+                    ready.at[group, some],
+                    out.at[some, pl.ds(group * GROUP, GROUP), :],
+                    sems.at[1 + len(stores)],
+                )
+            )
+            stores[-1].start()
     for store in stores:
         store.wait()
 
@@ -617,7 +612,7 @@
             pltpu.VMEM(smoothed.shape, jnp.bfloat16),
             pltpu.VMEM((SENSORS * GROUP, LANES), jnp.float32),
             pltpu.VMEM((columns // GROUP, SENSORS, GROUP, rows), jnp.bfloat16),
-            pltpu.SemaphoreType.DMA((3,)),
+            pltpu.SemaphoreType.DMA((1 + columns // GROUP * PIECES,)),
         ],
         compiler_params=pltpu.CompilerParams(vmem_limit_bytes=66_000_000),
         name="inverse_and_gain",
@@ -625,10 +620,10 @@
 
 
 def local(adjoint, seafloor_depth, sensor_row, sensor_column, noise_sigma):
-    smoothed, stacked = smoothed_and_gram(
+    smoothed, stacked = smoothed_and_operator(
         adjoint, seafloor_depth, sensor_row, sensor_column, noise_sigma
     )
-    return gains(all_reduced(stacked), smoothed)
+    return gains(stacked, smoothed)
 
 
 def solution(mesh):

time: 102 us -> 96.3 us (0.944)
  Pallas kernels: 102 us -> 95.9 us
    pallas_call x2 -> x1, Pallas kernels: 79.5 us -> 73.9 us  [smoothed_and_operator(): pl.pallas_call(smooth_kernel, out_shape=(jax.ShapeDtypeStruct((columns, r...]
where the time goes in v4:
time: 96.3 us; the launch traced here: 96.1 us
  Pallas kernels  95.9 us (100%)
    pallas_call x1, Pallas kernels, smoothed_and_operator(): pl.pallas_call(smooth_kernel, out_shape=(jax.ShapeDtypeStruct((columns, r...  73.9 us
    pallas_call x1, Pallas kernels, gains(): pl.pallas_call(gain_kernel, out_shape=jax.ShapeDtypeStruct((SENSORS, colu...  22 us

profile of v4, /device:TPU:1, one launch (start us, length us, event | category | flops | bytes accessed | tf_op | source)
XLA Modules:
  0.0 96.1 jit_solution(4216838171662997019)
XLA Ops:
  0.0 73.9 %smooth_and_reduce.1 = (bf16[32,128,640]{2,1,0:T(8,128)(2,1)}, f32[2304,128]{1,0:T(8,128)}) custom-call(bf16[600,32,128]{2,1,0:T(8,128)(2,1)} %adjoint.1, f32[32,128]{1,0:T(8,128)} %depth.1, s32[600]{0:T(1024)} %sensor_row.1, s32[600]{0:T(1024)} %sensor_column.1, f32[600]{0:T(1024)} %noise.1), custom_call_target="tpu_custom_call" | custom-call | tf_op jit(solution)/shard_map/smooth_and_reduce/pallas_call | solution.py:448
  73.9 22.0 %inverse_and_gain.1 = bf16[600,32,128]{2,1,0:T(8,128)(2,1)} custom-call(f32[2304,128]{1,0:T(8,128)} %get-tuple-element.7.stacked, bf16[32,128,640]{2,1,0:T(8,128)(2,1)} %get-tuple-element.8.smoothed_in), custom_call_target="tpu_custom_call" | custom-call | tf_op jit(solution)/shard_map/inverse_and_gain/pallas_call | solution.py:603
